TPU v7x, 256 devices: a whole 4x4x8 slice. The times are simulated.
256 devices in a mesh: dp: 4 (over x), ctx: 64 (over y, z, core).
Axes of the slice: x: 4, y: 4, z: 8, core: 2. Of those that a mesh axis runs over, the one named last changes fastest.
Arguments:
- doc_start: int32 [4, 64], P('dp'), may hold values from 0 to 8191, as said below
- doc_end: int32 [4, 64], P('dp'), may hold values from 1 to 8192, as said below
- modality: int32 [4, 64], P('dp'), may hold values from 0 to 1
- x_in: bfloat16 [4, 8192, 4096], P('dp', 'ctx'), may hold values from -5 to 5
- log_decay: float32 [4, 64, 8192], P('dp', None, 'ctx'), may hold values from -1 to 0, as said below
- b_in: bfloat16 [4, 8192, 512], P('dp', 'ctx'), may hold values from -2.5 to 2.5
- c_in: bfloat16 [4, 8192, 512], P('dp', 'ctx'), may hold values from -2.5 to 2.5
- gate_z: bfloat16 [4, 8192, 4096], P('dp', 'ctx'), may hold values from -40 to 40
- skip_d: float32 [64], replicated, may hold values from 0.5 to 2
- norm_gain: float32 [4096], replicated, may hold values from 0.25 to 1.75
- query: bfloat16 [4, 8192, 4096], P('dp', 'ctx'), may hold values from -5 to 5
- key: bfloat16 [4, 8192, 1024], P('dp', 'ctx'), may hold values from -5 to 5
- value: bfloat16 [4, 8192, 1024], P('dp', 'ctx'), may hold values from -12 to 12
- loss_weight: float32 [4, 8192], P('dp', 'ctx'), may hold values from 1 to 90
Outputs:
- mamba_mix: bfloat16 [4, 8192, 4096], P('dp', 'ctx')
- attn_mix: bfloat16 [4, 8192, 4096], P('dp', 'ctx')
- energy: float32 [2, 2], replicated
Inputs may be any that keep to these rules, and one draw needn't show every extreme that they name: `doc_start`: the documents of a sequence tile its positions in order: the first starts at 0, each ends where the next starts, the last ends at 8192. Each document has 1 to 384 positions, and every sequence has a document of exactly 384 positions. doc_end of a document is doc_start of the next one. `log_decay`: Negative.
All inputs are finite; a program needn't handle non-finite values.
Results may differ from a plain program's by a relative error of at most 0.0065.
Values may be sent and summed in bfloat16 or wider, within the bound.
A program may use at most 320 MiB of HBM per device.

v0:
```python
import jax
import jax.numpy as jnp
from jax import lax
from jax.sharding import PartitionSpec as P

H = 64
P_SIZE = 64
N = 128
NG = 4
AQ = 32
AK = 8
AD = 128
REACH = 3


norm_eps = 1e-05
masked_score = -1e30


def prefix(x, axis, combine, identity):
    devices, mine = (lax.axis_size(axis), lax.axis_index(axis))
    everything = jax.tree.map(lambda part: lax.all_gather(part, axis), x)
    start = jax.tree.map(
        lambda part, zero: jnp.broadcast_to(jnp.asarray(zero, part.dtype), part.shape), x, identity
    )

    def hop(k, before):
        reached = k < mine
        new = combine(before, jax.tree.map(lambda part: part[k], everything))
        return jax.tree.map(lambda a, b: jnp.where(reached, a, b), new, before)

    return lax.fori_loop(0, devices, hop, start)


def shifted(block, axis, distance):
    devices = range(lax.axis_size(axis))
    route = [(i - distance, i) for i in devices if i - distance in devices]
    return lax.ppermute(block, axis, route)


def doc_lookup(starts, ends, modes, positions):
    inside = (positions[:, None] >= starts[None, :]) & (positions[:, None] < ends[None, :])
    member = inside.astype(jnp.int32)
    labels = jnp.arange(starts.shape[0], dtype=jnp.int32)
    doc_of = jnp.sum(member * labels[None, :], axis=1)
    start_of = jnp.sum(member * starts[None, :], axis=1)
    mode_of = jnp.sum(member * modes[None, :], axis=1)
    present = jnp.sum(member, axis=1) > 0
    return (doc_of, start_of, mode_of, present)


def combine_states(earlier, later):
    return (earlier[0] * later[0], later[0][:, None, None] * earlier[1] + later[1])


def mamba_local(x_rows, decay_rows, b_rows, c_rows, doc_of):
    steps = x_rows.shape[0]
    per_group = H // NG
    running = jnp.cumsum(decay_rows, axis=1)
    order = jnp.arange(steps, dtype=jnp.int32)
    same_doc = (doc_of[:, None] == doc_of[None, :]) & (order[None, :] <= order[:, None])
    spread = running[:, :, None] - running[:, None, :]
    kernel = jnp.where(same_doc[None], jnp.exp(jnp.where(same_doc[None], spread, 0.0)), 0.0)
    b_grp = b_rows.reshape(steps, NG, N)
    c_grp = c_rows.reshape(steps, NG, N)
    intersection = jnp.einsum("tgn,sgn->gts", c_grp, b_grp, preferred_element_type=jnp.float32)
    mixing = (kernel.reshape(NG, per_group, steps, steps) * intersection[:, None]).astype(
        jnp.bfloat16
    )
    x_grp = x_rows.reshape(steps, NG, per_group, P_SIZE)
    inner = jnp.einsum("ghts,sghp->tghp", mixing, x_grp, preferred_element_type=jnp.float32)
    last_doc = doc_of == doc_of[steps - 1]
    tail = jnp.where(last_doc[None, :], jnp.exp(running[:, steps - 1 :] - running), 0.0)
    tail_rows = tail.reshape(NG, per_group, steps).transpose(2, 0, 1)[..., None]
    weighted = (x_grp.astype(jnp.float32) * tail_rows).astype(jnp.bfloat16)
    end_state = jnp.einsum("sghp,sgn->ghpn", weighted, b_grp, preferred_element_type=jnp.float32)
    return (inner, end_state.reshape(H, P_SIZE, N), running)


def mamba_finish(inner, state_in, running, carried, c_rows, x_rows, skip_d, gate_rows, norm_gain):
    steps = x_rows.shape[0]
    per_group = H // NG
    c_wide = c_rows.reshape(steps, NG, N).astype(jnp.float32)
    reached = jnp.einsum(
        "tgn,ghpn->tghp",
        c_wide,
        state_in.reshape(NG, per_group, P_SIZE, N),
        precision=lax.Precision.HIGHEST,
    )
    factor = (jnp.exp(running) * carried[None, :]).T.reshape(steps, NG, per_group)[..., None]
    x_wide = x_rows.reshape(steps, NG, per_group, P_SIZE).astype(jnp.float32)
    result = inner + reached * factor + skip_d.reshape(NG, per_group)[None, :, :, None] * x_wide
    gated = result.reshape(steps, NG, per_group * P_SIZE) * jax.nn.silu(
        gate_rows.reshape(steps, NG, per_group * P_SIZE).astype(jnp.float32)
    )
    square = jnp.mean(gated * gated, axis=-1, keepdims=True)
    normed = gated * lax.rsqrt(square + norm_eps) * norm_gain.reshape(NG, per_group * P_SIZE)[None]
    return normed.reshape(steps, H * P_SIZE).astype(jnp.bfloat16)


def attention_scores(q_head, k_head, scale):
    return jnp.einsum("rtd,kd->rtk", q_head, k_head, preferred_element_type=jnp.float32) * scale


def normalize(scores, allowed):
    scores = jnp.where(allowed[None], scores, masked_score)
    top = jnp.max(scores, axis=-1, keepdims=True)
    expo = jnp.exp(scores - top)
    return (expo / jnp.sum(expo, axis=-1, keepdims=True)).astype(jnp.bfloat16)


def shards(
    doc_start,
    doc_end,
    modality,
    x_in,
    log_decay,
    b_in,
    c_in,
    gate_z,
    skip_d,
    norm_gain,
    query,
    key,
    value,
    loss_weight,
):
    steps = x_in.shape[1]
    starts = doc_start[0]
    ends = doc_end[0]
    modes = modality[0]
    first_pos = lax.axis_index("ctx") * steps
    positions = first_pos + jnp.arange(steps, dtype=jnp.int32)
    doc_of, start_of, mode_of, present = doc_lookup(starts, ends, modes, positions)
    inner, end_state, running = mamba_local(x_in[0], log_decay[0], b_in[0], c_in[0], doc_of)
    carried = (start_of < first_pos).astype(jnp.float32)
    through = jnp.exp(running[:, steps - 1]) * carried[steps - 1]
    passed = prefix(
        (through, end_state),
        "ctx",
        combine_states,
        (jnp.ones_like(through), jnp.zeros_like(end_state)),
    )
    state_in = passed[1]
    mamba_mix = mamba_finish(
        inner, state_in, running, carried, c_in[0], x_in[0], skip_d, gate_z[0], norm_gain
    )
    received = {0: (key[0], value[0])}
    for offset in range(REACH, -REACH - 1, -1):
        if offset != 0:
            received[offset] = shifted((key[0], value[0]), "ctx", offset)
    key_parts = []
    value_parts = []
    pos_parts = []
    for offset in range(REACH, -REACH - 1, -1):
        key_parts.append(received[offset][0])
        value_parts.append(received[offset][1])
        pos_parts.append(positions - offset * steps)
    keys_all = jnp.concatenate(key_parts, axis=0)
    values_all = jnp.concatenate(value_parts, axis=0)
    key_pos = jnp.concatenate(pos_parts, axis=0)
    key_doc, key_start, key_mode, key_present = doc_lookup(starts, ends, modes, key_pos)
    allowed = (
        key_present[None, :]
        & (doc_of[:, None] == key_doc[None, :])
        & ((key_pos[None, :] <= positions[:, None]) | (mode_of[:, None] == 1))
    )
    ratio = AQ // AK
    scale = AD ** (-0.5)
    q_heads = query[0].reshape(steps, AK, ratio, AD).transpose(1, 2, 0, 3)
    k_heads = keys_all.reshape(-1, AK, AD).transpose(1, 0, 2)
    v_heads = values_all.reshape(-1, AK, AD).transpose(1, 0, 2)

    def per_head(operands):
        probs = normalize(attention_scores(operands[0], operands[1], scale), allowed)
        return jnp.einsum("rtk,kd->rtd", probs, operands[2], preferred_element_type=jnp.float32)

    heads_out = lax.map(per_head, (q_heads, k_heads, v_heads))
    attn_mix = heads_out.transpose(2, 0, 1, 3).reshape(steps, AQ * AD).astype(jnp.bfloat16)
    count = float(lax.axis_size("dp") * lax.axis_size("ctx") * steps)
    mamba_energy = jnp.mean(jnp.square(mamba_mix.astype(jnp.float32)), axis=-1)
    attn_energy = jnp.mean(jnp.square(attn_mix.astype(jnp.float32)), axis=-1)
    mode_hot = jnp.stack([mode_of == 0, mode_of == 1]).astype(jnp.float32) * loss_weight[0][None, :]
    terms = (
        jnp.stack(
            [
                jnp.sum(mode_hot * mamba_energy[None, :], axis=1),
                jnp.sum(mode_hot * attn_energy[None, :], axis=1),
            ],
            axis=1,
        )
        / count
    )
    energy = lax.psum(terms, ("dp", "ctx"))
    return (mamba_mix[None], attn_mix[None], energy)


def solution(mesh):
    placed = (
        P("dp", None),
        P("dp", None),
        P("dp", None),
        P("dp", "ctx", None),
        P("dp", None, "ctx"),
        P("dp", "ctx", None),
        P("dp", "ctx", None),
        P("dp", "ctx", None),
        P(),
        P(),
        P("dp", "ctx", None),
        P("dp", "ctx", None),
        P("dp", "ctx", None),
        P("dp", "ctx"),
    )
    return jax.shard_map(
        shards,
        mesh=mesh,
        in_specs=placed,
        out_specs=(P("dp", "ctx", None), P("dp", "ctx", None), P()),
        check_vma=False,
    )
```

profile of v0, /device:TPU:1, one launch (start us, length us, event | category | flops | bytes accessed | tf_op | source)
XLA Modules:
  0.0 779.9 jit_solution(10819306167020658213)
XLA Ops:
  16.8 7.0 collective-permute-start
  23.8 3.5 collective-permute-start.1
  29.3 3.1 collective-permute-start.3
  32.6 5.3 collective-permute-start.6
  39.1 3.3 fusion.49
  42.9 2.3 copy.67
  49.2 253.3 %all-reduce = f32[4096]{0:T(1024)} all-reduce(f32[4096]{0:T(1024)} %dynamic-update-slice), channel_id=2, replica_groups=mesh['dp'=4,'ctx'=64] {'ctx'}, use_global_device_ids=true, to_apply=%add | all-reduce | flops 4096 | bytes 32768
  303.9 2.6 copy.65
  313.9 9.8 %collective-permute-start.7 = (bf16[128,1024]{0,1:T(8,128)(2,1)S(1)}, bf16[128,1024]{0,1:T(8,128)(2,1)S(1)}, u32[]{:S(2)}, u32[]{:S(2)}) collective-permute-start(bf16[128,1024]{0,1:T(8,128)(2,1)S(1)} %bitcast.135), channel_id=1, source_target_pairs={{0,2},{1,3},{2,4},{3,5},{4,6},{5,7},{6,8},{7,9},{8,10},{9,11},{10,... | collective-permute-start | bytes 786440 | tf_op jit(solution)/shard_map/ppermute | solution.py:38
  333.6 5.9 collective-permute-done.5
  341.0 3.0 collective-permute-done.8
  344.1 2.9 collective-permute-done.9
  347.1 2.5 collective-permute-done.10
  349.7 23.4 %collective-permute-done.11 = bf16[128,1024]{0,1:T(8,128)(2,1)S(1)} collective-permute-done((bf16[128,1024]{0,1:T(8,128)(2,1)S(1)}, bf16[128,1024]{0,1:T(8,128)(2,1)S(1)}, u32[]{:S(2)}, u32[]{:S(2)}) %collective-permute-start.11) | collective-permute-done | bytes 262176 | tf_op jit(solution)/shard_map/ppermute | solution.py:38
  374.5 47.5 %while.25 = (s32[]{:T(128)}, bf16[8,4,128,128]{3,2,1,0:T(8,128)(2,1)}, bf16[8,4,128,128]{2,3,1,0:T(8,128)(2,1)}, bf16[8,896,128]{1,2,0:T(8,128)(2,1)}, bf16[8,89...) while((s32[]{:T(128)}, ...), condition=%wide.region_12.13_spmd.clone, body=%wide.region_9.12_spmd.clone.sunk | while | flops 357026048 | bytes 1572981 | solution.py:178
  377.3 3.1 fusion.90
  383.2 3.1 fusion.90
  389.1 3.4 fusion.90
  395.3 3.1 fusion.90
  401.2 3.2 fusion.90
  407.1 3.1 fusion.90
  413.0 3.1 fusion.90
  418.9 3.2 fusion.90
  422.0 3.1 copy.75
  425.1 2.6 convert_element_type.86
  429.3 68.0 %all-gather.3.cloned.1.call-done = f32[64,64,64,128]{3,2,1,0:T(8,128)} async-done(((f32[1,64,64,128]{3,2,1,0:T(8,128)}), f32[64,64,64,128]{3,2,1,0:T(8,128)}) %all-gather.3.cloned.1.call-update) | async-done | bytes 134217744 | tf_op jit(solution)/shard_map/all_gather | solution.py:22
  497.2 178.1 %while.26 = (s32[]{:T(128)}, f32[64,64,128]{2,1,0:T(8,128)S(1)}, s32[]{:T(128)}, f32[64,64]{1,0:T(8,128)}, f32[64,64,64,128]{3,2,1,0:T(8,128)}, /*index=5*/s32[]{:T(128)}, s32[]{:T(128)}) while((s32[]{:T(128)}, f32[64,64,128]{2,1,0:T(8,128)S(1)}, s32[]{:T(128)}, f32[64,64]{1,0:T(8,128)}, f32[64,64,64,128]{3,2,1,0:T(8,128)}, ...), condition=%wide.region_4.5_spmd.clone, body=%wide.region_3.0_spmd.clone.sunk | while | flops 2097156 | bytes 6292329 | solution.py:32
  675.4 5.5 multiply_reduce_fusion.2
  681.9 79.8 %psum.7 = f32[2,2]{0,1:T(2,128)S(1)} all-reduce(f32[2,2]{0,1:T(2,128)S(1)} %maximum_multiply_fusion), channel_id=1, replica_groups=mesh['dp'=4,'ctx'=64] {'dp','ctx'}, use_global_device_ids=true, to_apply=%region_17.18 | all-reduce | flops 4 | bytes 32 | tf_op jit(solution)/shard_map/psum | solution.py:194
  764.0 2.7 mul.239
  766.8 3.0 copy.64
  769.8 3.3 multiply_convert_fusion.3
  (255 shorter events, 241.8 us)
Async XLA Ops:
  7.2 6.9 copy-start.4
  7.2 490.1 %all-gather.3.cloned.1.call-start = ((), (), s32[]{:S(2)}) async-start(), calls=%async_computation | async-start | bytes 136314880 | tf_op jit(solution)/shard_map/all_gather | solution.py:22
  7.2 8.7 %copy-start.10 = (s32[128]{0:T(128)}, s32[128]{0:T(128)S(1)}, u32[]{:S(2)}) copy-start(s32[128]{0:T(128)S(1)} %get-tuple-element.400) | copy-start | bytes 1540
  14.2 1.8 copy-start.1
  15.9 16.5 %copy-start.2 = (bf16[1,128,1024]{2,1,0:T(8,128)(2,1)S(1)}, bf16[1,128,1024]{2,1,0:T(8,128)(2,1)}, u32[]{:S(2)}) copy-start(bf16[1,128,1024]{2,1,0:T(8,128)(2,1)} %param.30) | copy-start | bytes 786436
  15.9 21.9 %copy-start.5 = (bf16[1,128,512]{2,1,0:T(8,128)(2,1)S(1)}, bf16[1,128,512]{2,1,0:T(8,128)(2,1)}, u32[]{:S(2)}) copy-start(bf16[1,128,512]{2,1,0:T(8,128)(2,1)} %param.24) | copy-start | bytes 393220
  15.9 22.1 %copy-start.14 = (s32[1,64]{1,0:T(1,128)S(1)}, s32[1,64]{1,0:T(1,128)}, u32[]{:S(2)}) copy-start(s32[1,64]{1,0:T(1,128)} %param.19) | copy-start | bytes 772
  15.9 22.1 %copy-start.15 = (s32[1,64]{1,0:T(1,128)S(1)}, s32[1,64]{1,0:T(1,128)}, u32[]{:S(2)}) copy-start(s32[1,64]{1,0:T(1,128)} %param.18) | copy-start | bytes 772
  16.8 292.4 %collective-permute-start = (bf16[128,1024]{0,1:T(8,128)(2,1)}, bf16[128,1024]{0,1:T(8,128)(2,1)}, u32[]{:S(2)}, u32[]{:S(2)}) collective-permute-start(bf16[128,1024]{0,1:T(8,128)(2,1)} %bitcast.21), channel_id=1, source_target_pairs={{0,3},{1,4},{2,5},{3,6},{4,7},{5,8},{6,9},{7,10},{8,11},{9,12},{10... | collective-permute-start | bytes 786440 | tf_op jit(solution)/shard_map/ppermute | solution.py:38
  23.8 290.1 %collective-permute-start.1 = (bf16[128,1024]{0,1:T(8,128)(2,1)}, bf16[128,1024]{0,1:T(8,128)(2,1)}, u32[]{:S(2)}, u32[]{:S(2)}) collective-permute-start(bf16[128,1024]{0,1:T(8,128)(2,1)} %bitcast.21), channel_id=1, source_target_pairs={{0,2},{1,3},{2,4},{3,5},{4,6},{5,7},{6,8},{7,9},{8,10},{9,11},{10,... | collective-permute-start | bytes 786440 | tf_op jit(solution)/shard_map/ppermute | solution.py:38
  27.4 297.4 %collective-permute-start.2 = (bf16[128,1024]{0,1:T(8,128)(2,1)}, bf16[128,1024]{0,1:T(8,128)(2,1)}, u32[]{:S(2)}, u32[]{:S(2)}) collective-permute-start(bf16[128,1024]{0,1:T(8,128)(2,1)} %bitcast.21), channel_id=1, source_target_pairs={{0,1},{1,2},{2,3},{3,4},{4,5},{5,6},{6,7},{7,8},{8,9},{9,10},{10,1... | collective-permute-start | bytes 786440 | tf_op jit(solution)/shard_map/ppermute | solution.py:38
  29.3 299.7 %collective-permute-start.3 = (bf16[128,1024]{0,1:T(8,128)(2,1)}, bf16[128,1024]{0,1:T(8,128)(2,1)}, u32[]{:S(2)}, u32[]{:S(2)}) collective-permute-start(bf16[128,1024]{0,1:T(8,128)(2,1)} %bitcast.21), channel_id=1, source_target_pairs={{1,0},{2,1},{3,2},{4,3},{5,4},{6,5},{7,6},{8,7},{9,8},{10,9},{11,1... | collective-permute-start | bytes 786440 | tf_op jit(solution)/shard_map/ppermute | solution.py:38
  32.6 279.0 %collective-permute-start.6 = (bf16[128,1024]{0,1:T(8,128)(2,1)S(1)}, bf16[128,1024]{0,1:T(8,128)(2,1)}, u32[]{:S(2)}, u32[]{:S(2)}) collective-permute-start(bf16[128,1024]{0,1:T(8,128)(2,1)S(1)} %bitcast.134), channel_id=1, source_target_pairs={{0,3},{1,4},{2,5},{3,6},{4,7},{5,8},{6,9},{7,10},{8,11},{9,12},{10... | collective-permute-start | bytes 786440 | tf_op jit(solution)/shard_map/ppermute | solution.py:38
  309.3 23.0 %collective-permute-start.4 = (bf16[128,1024]{0,1:T(8,128)(2,1)}, bf16[128,1024]{0,1:T(8,128)(2,1)S(1)}, u32[]{:S(2)}, u32[]{:S(2)}) collective-permute-start(bf16[128,1024]{0,1:T(8,128)(2,1)} %bitcast.21), channel_id=1, source_target_pairs={{2,0},{3,1},{4,2},{5,3},{6,4},{7,5},{8,6},{9,7},{10,8},{11,9},{12,... | collective-permute-start | bytes 786440 | tf_op jit(solution)/shard_map/ppermute | solution.py:38
  311.6 27.9 %collective-permute-start.5 = (bf16[128,1024]{0,1:T(8,128)(2,1)}, bf16[128,1024]{0,1:T(8,128)(2,1)S(1)}, u32[]{:S(2)}, u32[]{:S(2)}) collective-permute-start(bf16[128,1024]{0,1:T(8,128)(2,1)} %bitcast.21), channel_id=1, source_target_pairs={{3,0},{4,1},{5,2},{6,3},{7,4},{8,5},{9,6},{10,7},{11,8},{12,9},{13... | collective-permute-start | bytes 786440 | tf_op jit(solution)/shard_map/ppermute | solution.py:38
  313.9 27.0 %collective-permute-start.7 = (bf16[128,1024]{0,1:T(8,128)(2,1)S(1)}, bf16[128,1024]{0,1:T(8,128)(2,1)S(1)}, u32[]{:S(2)}, u32[]{:S(2)}) collective-permute-start(bf16[128,1024]{0,1:T(8,128)(2,1)S(1)} %bitcast.135), channel_id=1, source_target_pairs={{0,2},{1,3},{2,4},{3,5},{4,6},{5,7},{6,8},{7,9},{8,10},{9,11},{10,... | collective-permute-start | bytes 786440 | tf_op jit(solution)/shard_map/ppermute | solution.py:38
  324.8 19.2 %collective-permute-start.8 = (bf16[128,1024]{0,1:T(8,128)(2,1)S(1)}, bf16[128,1024]{0,1:T(8,128)(2,1)S(1)}, u32[]{:S(2)}, u32[]{:S(2)}) collective-permute-start(bf16[128,1024]{0,1:T(8,128)(2,1)S(1)} %bitcast.136), channel_id=1, source_target_pairs={{0,1},{1,2},{2,3},{3,4},{4,5},{5,6},{6,7},{7,8},{8,9},{9,10},{10,1... | collective-permute-start | bytes 786440 | tf_op jit(solution)/shard_map/ppermute | solution.py:38
  329.0 18.1 %collective-permute-start.9 = (bf16[128,1024]{0,1:T(8,128)(2,1)S(1)}, bf16[128,1024]{0,1:T(8,128)(2,1)S(1)}, u32[]{:S(2)}, u32[]{:S(2)}) collective-permute-start(bf16[128,1024]{0,1:T(8,128)(2,1)S(1)} %bitcast.137), channel_id=1, source_target_pairs={{1,0},{2,1},{3,2},{4,3},{5,4},{6,5},{7,6},{8,7},{9,8},{10,9},{11,1... | collective-permute-start | bytes 786440 | tf_op jit(solution)/shard_map/ppermute | solution.py:38
  332.2 17.4 %collective-permute-start.10 = (bf16[128,1024]{0,1:T(8,128)(2,1)S(1)}, bf16[128,1024]{0,1:T(8,128)(2,1)S(1)}, u32[]{:S(2)}, u32[]{:S(2)}) collective-permute-start(bf16[128,1024]{0,1:T(8,128)(2,1)S(1)} %bitcast.138), channel_id=1, source_target_pairs={{2,0},{3,1},{4,2},{5,3},{6,4},{7,5},{8,6},{9,7},{10,8},{11,9},{12,... | collective-permute-start | bytes 786440 | tf_op jit(solution)/shard_map/ppermute | solution.py:38
  339.5 33.6 %collective-permute-start.11 = (bf16[128,1024]{0,1:T(8,128)(2,1)S(1)}, bf16[128,1024]{0,1:T(8,128)(2,1)S(1)}, u32[]{:S(2)}, u32[]{:S(2)}) collective-permute-start(bf16[128,1024]{0,1:T(8,128)(2,1)S(1)} %bitcast.139), channel_id=1, source_target_pairs={{3,0},{4,1},{5,2},{6,3},{7,4},{8,5},{9,6},{10,7},{11,8},{12,9},{13... | collective-permute-start | bytes 786440 | tf_op jit(solution)/shard_map/ppermute | solution.py:38
  340.9 32.3 %copy-start.8 = (bf16[896,8,128]{0,2,1:T(8,128)(2,1)}, bf16[896,8,128]{0,2,1:T(8,128)(2,1)S(1)}, u32[]{:S(2)}) copy-start(bf16[896,8,128]{0,2,1:T(8,128)(2,1)S(1)} %constant_dynamic-update-slice_fusion) | copy-start | bytes 5505028
  373.2 1.3 copy-start.7
  497.2 178.1 %copy-start.9 = (f32[64,128]{1,0:T(8,128)S(1)}, f32[64,128]{1,0:T(8,128)}, u32[]{:S(2)}) copy-start(f32[64,128]{1,0:T(8,128)} %exponential_multiply_fusion) | copy-start | bytes 98308
  497.2 178.1 %copy-start.11 = (f32[4,16]{1,0:T(4,128)S(1)}, f32[4,16]{1,0:T(4,128)}, u32[]{:S(2)}) copy-start(f32[4,16]{1,0:T(4,128)} %mul.230) | copy-start | bytes 772
  675.4 5.5 copy-start.3
  680.8 0.8 copy-start.12
  680.8 0.8 copy-start.13
  680.8 0.8 copy-start.16
  766.7 3.0 copy-start
  766.7 3.0 copy-start.6
Sparse Core Ops, SparseCore 0:
  16.1 481.0 all-gather.2
where the time goes:
time: 786 us; the launch traced here: 780 us
  blocking collectives  333 us (42%)
  other arithmetic  150 us (19%)
  waiting for transfers between devices  106 us (13%)
  local copies, waits for them, and re-layouts  82 us (10%)
  matrix products  51.5 us (7%)
  starting transfers between devices  40.2 us (5%)
  between operations  15.2 us (2%)
    unnamed x1, blocking collectives  253 us
    select_n x64, other arithmetic, hop(): return jax.tree.map(lambda a, b: jnp.where(reached, a, b), new, before)  133 us
    psum x1, blocking collectives, shards(): energy = lax.psum(terms, ('dp', 'ctx'))  79.8 us
    all_gather x1, waiting for transfers between devices, prefix(): everything = jax.tree.map(lambda part: lax.all_gather(part, axis), x)  68 us
    mul x64, local copies, waits for them, and re-layouts, combine_states(): later[0][:, None, None] * earlier[1] + later[1]  43.9 us
    ppermute x12, starting transfers between devices, shifted(): return lax.ppermute(block, axis, route)  40.2 us
    ppermute x12, waiting for transfers between devices, shifted(): return lax.ppermute(block, axis, route)  37.8 us
    dot_general x8, matrix products, per_head(): jnp.einsum('rtk,kd->rtd', probs, operands[2], preferred_element_type=jnp....  25.4 us
  transfers between devices with their start and end apart: 13, of which 6 were waited for; matrix products, arithmetic and copies ran while one was open for 10% of the time, Pallas kernels for 0%

commit v1 on v0

v1 whole, which is shorter than its diff:
```python
import functools
import math

import jax
import jax.numpy as jnp
from jax import lax
from jax.experimental import pallas as pl
from jax.experimental.pallas import tpu as pltpu
from jax.sharding import PartitionSpec as P

H = 64
P_SIZE = 64
N = 128
NG = 4
AQ = 32
AK = 8
AD = 128
REACH = 3
TOK = 128
WIN = (2 * REACH + 1) * TOK
GW = (H // NG) * P_SIZE
HPG = H // NG

norm_eps = 1e-05
masked_score = -1e30
MESH = pl.DeviceIdType.MESH
HIGHEST = lax.Precision.HIGHEST
f32 = jnp.float32
bf16 = jnp.bfloat16
NT = (((1,), (1,)), ((), ()))
TN = (((0,), (0,)), ((), ()))
NN = (((1,), (0,)), ((), ()))


def dot(a, b, dims=NN, precision=None):
    return lax.dot_general(a, b, dims, precision=precision, preferred_element_type=f32)


def iota(shape, axis):
    return lax.broadcasted_iota(jnp.int32, shape, axis)


def body(
    n_dp,
    n_ctx,
    near,
    starts_ref,
    ends_ref,
    modes_ref,
    x_ref,
    decay_ref,
    b_ref,
    c_ref,
    gate_ref,
    skip_ref,
    gain_ref,
    q_ref,
    k_ref,
    v_ref,
    lw_ref,
    mamba_ref,
    attn_ref,
    energy_ref,
    kbuf,
    vbuf,
    abuf,
    bbuf,
    sbuf,
    ebuf,
    ewide,
    tbuf,
    tsend,
    fx,
    res,
    bias,
    mmask,
    lastm,
    carm,
    hot,
    runc,
    runr,
    acc,
    lsum,
    mtop,
    esq,
    e1,
    e2,
    e3,
    kv_send,
    kv_recv,
    st_send,
    a_recv,
    b_recv,
    s_send,
    s_recv,
    rel1,
    rel2,
    en_send,
    en_recv,
):
    b = lax.axis_index("ctx")
    dp = lax.axis_index("dp")
    core = b % 2
    row, lane_pos = b // near, b % near
    n_row = n_ctx // near
    seq = n_ctx * TOK
    first = b * TOK
    even, odd = core == 0, core == 1

    def peer(i):
        return {"ctx": i}

    barrier = pltpu.get_barrier_semaphore()

    def greet(device):
        pl.semaphore_signal(barrier, inc=1, device_id=device, device_id_type=MESH)

    @pl.loop(1, near)
    def _(k):
        greet({"ctx": row * near + (lane_pos + k) % near})

    for k in range(1, n_row):
        greet({"ctx": ((row + k) % n_row) * near + lane_pos})
    for k in range(1, n_dp):
        greet({"dp": (dp + k) % n_dp})
    count = near - 1 + n_row - 1 + n_dp - 1
    for d in (-2, -1, 1, 2):
        ok = (b + d >= 0) & (b + d < n_ctx)

        @pl.when(ok)
        def _(d=d):
            greet({"ctx": b + d})

        count = count + jnp.where(ok, 1, 0)

    st_row = starts_ref[...].astype(f32)
    en_row = ends_ref[...].astype(f32)
    mo_row = modes_ref[...].astype(f32)
    docs = st_row.shape[1]
    diag = iota((docs, docs), 0) == iota((docs, docs), 1)

    def column(r):
        return jnp.sum(jnp.where(diag, r, 0.0), axis=1, keepdims=True)

    st_col, en_col, mo_col = column(st_row), column(en_row), column(mo_row)
    first_f = first.astype(f32)
    pos_col = first_f + iota((TOK, 1), 0).astype(f32)
    below = st_row <= pos_col
    member = jnp.where(below & (pos_col < en_row), 1.0, 0.0)
    cnt_col = jnp.sum(jnp.where(below, 1.0, 0.0), axis=1, keepdims=True)
    begin_col = jnp.sum(member * st_row, axis=1, keepdims=True)
    mode_col = jnp.sum(member * mo_row, axis=1, keepdims=True)
    key_pos = first_f - float(REACH * TOK) + iota((1, WIN), 1).astype(f32)
    cnt_row = jnp.sum(jnp.where(st_col <= key_pos, 1.0, 0.0), axis=0, keepdims=True)
    present = (key_pos >= 0.0) & (key_pos < float(seq))
    same = (cnt_row == cnt_col) & present
    allowed = same & ((key_pos <= pos_col) | (mode_col == 1.0))
    bias[...] = jnp.where(allowed, 0.0, masked_score)
    own = slice(REACH * TOK, (REACH + 1) * TOK)
    own_same = cnt_row[:, own] == cnt_col
    mmask[...] = jnp.where(own_same & (iota((TOK, TOK), 1) <= iota((TOK, TOK), 0)), 1.0, 0.0)
    lastm[...] = jnp.broadcast_to(
        jnp.where(cnt_col == cnt_col[TOK - 1 :, :], 1.0, 0.0), (TOK, TOK)
    )
    carried = jnp.where(begin_col < first_f, 1.0, 0.0)
    carm[...] = jnp.broadcast_to(carried, (TOK, TOK))
    own_pos = key_pos[:, own]
    own_member = jnp.where((st_col <= own_pos) & (own_pos < en_col), 1.0, 0.0)
    mode_row = jnp.sum(own_member * mo_col, axis=0, keepdims=True)
    which = iota((8, TOK), 0).astype(f32)
    hot[...] = jnp.where(which == mode_row, lw_ref[...], 0.0)

    upto = jnp.where(iota((TOK, TOK), 0) >= iota((TOK, TOK), 1), 1.0, 0.0)
    decay = decay_ref[...]
    runr[...] = dot(decay, upto, NT, HIGHEST)
    for g in range(NG):
        runc[g, :, :HPG] = dot(upto, decay[g * HPG : (g + 1) * HPG, :], NT, HIGHEST)
    esq[...] = jnp.zeros_like(esq)

    for i in (0, 1, 2, 4, 5, 6):

        @pl.when((b - REACH + i < 0) | (b - REACH + i >= n_ctx))
        def _(i=i):
            kbuf[i] = jnp.zeros((TOK, AK * AD), bf16)
            vbuf[i] = jnp.zeros((TOK, AK * AD), bf16)

    @pl.when(b == 0)
    def _():
        abuf[...] = jnp.zeros_like(abuf)
        sbuf[...] = jnp.zeros_like(sbuf)

    @pl.when(b < 3)
    def _():
        bbuf[...] = jnp.zeros_like(bbuf)

    pl.semaphore_wait(barrier, count)

    def remote(src, dst, send, recv, to):
        return pltpu.make_async_remote_copy(
            src_ref=src,
            dst_ref=dst,
            send_sem=send,
            recv_sem=recv,
            device_id=peer(to),
            device_id_type=MESH,
        )

    def kv(which_send, from_slot, to_slot, to):
        k_src = k_ref if from_slot is None else kbuf.at[from_slot]
        v_src = v_ref if from_slot is None else vbuf.at[from_slot]
        return (
            remote(k_src, kbuf.at[to_slot], kv_send.at[which_send, 0], kv_recv.at[to_slot, 0], to),
            remote(v_src, vbuf.at[to_slot], kv_send.at[which_send, 1], kv_recv.at[to_slot, 1], to),
        )

    fwd2, bwd2 = b + 2 < n_ctx, b - 2 >= 0
    fwd1, bwd1 = b + 1 < n_ctx, b - 1 >= 0
    has_r2, has_l2 = bwd2, fwd2
    sends = [
        (fwd2, lambda: kv(0, None, 1, b + 2)),
        (bwd2, lambda: kv(1, None, 5, b - 2)),
        (even, lambda: kv(2, None, 2, b + 1)),
        (odd, lambda: kv(2, None, 4, b - 1)),
    ]
    relays = [
        (has_r2 & even, lambda: kv(3, 1, 0, b + 1)),
        (has_r2 & odd, lambda: kv(3, 1, 2, b - 1)),
        (has_l2 & even, lambda: kv(4, 5, 4, b + 1)),
        (has_l2 & odd, lambda: kv(4, 5, 6, b - 1)),
        (has_r2 & odd & fwd1, lambda: kv(5, 1, 0, b + 1)),
        (has_l2 & even & bwd1, lambda: kv(5, 5, 6, b - 1)),
    ]

    def start(plan):
        for when, make in plan:

            @pl.when(when)
            def _(make=make):
                for copy in make():
                    copy.start()

    def sent(plan):
        for when, make in plan:

            @pl.when(when)
            def _(make=make):
                for copy in make():
                    copy.wait_send()

    def arrived(slot):
        @pl.when((b - REACH + slot >= 0) & (b - REACH + slot < n_ctx))
        def _():
            for copy in kv(0, None, slot, b):
                copy.wait_recv()

    start(sends)

    lane = iota((TOK, TOK), 1)
    left = lane < P_SIZE

    def state_copy(g):
        return remote(ebuf.at[g], abuf.at[g], st_send.at[g], a_recv.at[g], b + 1)

    def scale_copy():
        return remote(tsend, sbuf, s_send, s_recv, b + 1)

    @pl.loop(0, NG)
    def _(g):
        cols = runc[g]
        parts = []
        for pair in range(HPG // 2):
            at = slice(pair * TOK, (pair + 1) * TOK)
            c0 = jnp.broadcast_to(cols[:, 2 * pair : 2 * pair + 1], (TOK, TOK))
            c1 = jnp.broadcast_to(cols[:, 2 * pair + 1 : 2 * pair + 2], (TOK, TOK))
            both = jnp.where(left, c0, c1)
            end = both[TOK - 1 :, :]
            fx[g, :, at] = jnp.exp(both) * carm[...]
            tbuf[g, :, at] = jnp.exp(end) * carm[TOK - 1 :, :]
            tail = jnp.exp(end - both) * lastm[...]
            lanes = pl.ds(pl.multiple_of(g * GW + pair * TOK, TOK), TOK)
            parts.append((x_ref[:, lanes].astype(f32) * tail).astype(bf16))
        weighted = jnp.concatenate(parts, axis=1)
        b_grp = b_ref[:, pl.ds(pl.multiple_of(g * N, N), N)]
        e = dot(b_grp, weighted, TN)
        ewide[g] = e
        ebuf[g] = e.astype(bf16)

        @pl.when(even)
        def _():
            state_copy(g).start()

    @pl.when(even)
    def _():
        tsend[...] = tbuf[...]
        scale_copy().start()

    @pl.when(odd)
    def _():
        scale_copy().wait_recv()
        tsend[...] = tbuf[...] * sbuf[...]

        @pl.when(fwd1)
        def _():
            scale_copy().start()

    def combine(g):
        state_copy(g).wait_recv()
        ebuf[g] = (ewide[g] + tbuf[g] * abuf[g].astype(f32)).astype(bf16)

        @pl.when(fwd1)
        def _():
            state_copy(g).start()

    @pl.when(odd)
    def _():
        combine(0)
        combine(1)

    @pl.loop(0, NG)
    def _(g):
        lanes_n = pl.ds(pl.multiple_of(g * N, N), N)
        both_docs = dot(c_ref[:, lanes_n], b_ref[:, lanes_n], NT) * mmask[...]
        cols = runc[g]
        rows = runr[pl.ds(pl.multiple_of(g * HPG, HPG), HPG), :]
        for pair in range(HPG // 2):
            at = slice(pair * TOK, (pair + 1) * TOK)
            mixes = []
            for h in (2 * pair, 2 * pair + 1):
                spread = cols[:, h : h + 1] - rows[h : h + 1, :]
                mixes.append((jnp.exp(jnp.minimum(spread, 0.0)) * both_docs).astype(bf16))
            xp = x_ref[:, pl.ds(pl.multiple_of(g * GW + pair * TOK, TOK), TOK)]
            zero = jnp.zeros_like(xp)
            split = jnp.concatenate([jnp.where(left, xp, zero), jnp.where(left, zero, xp)], axis=0)
            inner = dot(jnp.concatenate(mixes, axis=1), split)
            h0 = g * HPG + 2 * pair
            skip = jnp.where(left, skip_ref[h0], skip_ref[h0 + 1])
            res[g, :, at] = inner + skip * xp.astype(f32)

    arrived(1)
    arrived(5)
    start(relays)

    @pl.when(odd)
    def _():
        combine(2)
        combine(3)

    ratio = AQ // AK
    scale = AD ** (-0.5) * math.log2(math.e)

    def attend(j, slots):
        heads = pl.ds(pl.multiple_of(j * AD, AD), AD)
        q = jnp.concatenate(
            [
                q_ref[:, pl.ds(pl.multiple_of(j * ratio * AD + r * AD, AD), AD)]
                for r in range(ratio)
            ],
            axis=0,
        )
        keys = jnp.concatenate(
            [(k_ref[:, heads] if i == REACH else kbuf[i, :, heads]) for i in slots], axis=0
        )
        values = jnp.concatenate(
            [(v_ref[:, heads] if i == REACH else vbuf[i, :, heads]) for i in slots], axis=0
        )
        masks = jnp.concatenate([bias[:, i * TOK : (i + 1) * TOK] for i in slots], axis=1)
        s = dot(q, keys, NT) * scale
        s = s.reshape(ratio, TOK, len(slots) * TOK) + masks[None]
        s = s.reshape(ratio * TOK, len(slots) * TOK)
        wide = jnp.concatenate([values, jnp.ones_like(values)], axis=1)
        return s, wide

    near_slots, far_slots = (1, 2, 3, 4, 5), (0, 6)
    arrived(2)
    arrived(4)

    def relay_state(g):
        up = remote(abuf.at[g], bbuf.at[g], rel1.at[g], b_recv.at[g], b + 1)
        over = remote(abuf.at[g], bbuf.at[g], rel2.at[g], b_recv.at[g], b + 2)
        return up, over

    def pass_on(g):
        @pl.when(even & bwd1)
        def _():
            state_copy(g).wait_recv()
            up, over = relay_state(g)

            @pl.when(fwd2)
            def _():
                over.start()

            up.start()

    @pl.loop(0, NG)
    def _(g):
        for half in range(AK // NG):
            j = g * (AK // NG) + half
            s, wide = attend(j, near_slots)
            top = jnp.max(s, axis=1, keepdims=True)
            p = jnp.exp2(s - top).astype(bf16)
            o = dot(p, wide)
            acc[j] = o[:, :AD]
            lsum[j] = o[:, AD:]
            mtop[j] = jnp.broadcast_to(top, (ratio * TOK, AD))
        pass_on(g)

    arrived(0)
    arrived(6)

    @pl.loop(0, AK)
    def _(j):
        s, wide = attend(j, far_slots)
        before = mtop[j]
        top = jnp.maximum(before, jnp.max(s, axis=1, keepdims=True))
        p = jnp.exp2(s - jnp.concatenate([top] * len(far_slots), axis=1)).astype(bf16)
        o = dot(p, wide)
        fade = jnp.exp2(before - top)
        total = lsum[j] * fade + o[:, AD:]
        out = ((acc[j] * fade + o[:, :AD]) / total).astype(bf16)
        square = jnp.zeros((TOK, AD), f32)
        for r in range(ratio):
            piece = out[r * TOK : (r + 1) * TOK]
            attn_ref[:, pl.ds(pl.multiple_of(j * ratio * AD + r * AD, AD), AD)] = piece
            wide_piece = piece.astype(f32)
            square = square + wide_piece * wide_piece
        esq[1] = esq[1] + square

    @pl.when(odd)
    def _():
        pass

    @pl.when(even & bwd1)
    def _():
        scale_copy().wait_recv()

    @pl.loop(0, NG)
    def _(g):
        @pl.when(b >= 3)
        def _():
            remote(bbuf.at[g], bbuf.at[g], rel1.at[g], b_recv.at[g], b).wait_recv()

        c_grp = c_ref[:, pl.ds(pl.multiple_of(g * N, N), N)]
        reached = dot(c_grp, abuf[g]) + dot(c_grp, bbuf[g]) * sbuf[g]
        lanes = pl.ds(pl.multiple_of(g * GW, GW), GW)
        result = res[g] + reached * fx[g]
        z = gate_ref[:, lanes].astype(f32)
        gated = result * (z / (1.0 + jnp.exp(-z)))
        square = jnp.sum(gated * gated, axis=1, keepdims=True) * (1.0 / GW)
        mixed = (gated * lax.rsqrt(square + norm_eps) * gain_ref[:, lanes]).astype(bf16)
        mamba_ref[:, lanes] = mixed
        again = mixed.astype(f32)
        again = again * again
        part = again[:, :TOK]
        for i in range(1, GW // TOK):
            part = part + again[:, i * TOK : (i + 1) * TOK]
        esq[0] = esq[0] + part

    per_mode = [
        jnp.sum(dot(hot[...], esq[i], NN, HIGHEST), axis=1, keepdims=True) for i in range(2)
    ]
    small = iota((8, TOK), 1)
    denom = float(n_dp * n_ctx * TOK) * float(H * P_SIZE)
    mine = jnp.where(small == 0, per_mode[0], jnp.where(small == 1, per_mode[1], 0.0)) / denom

    def exchange(buf, size, me, base, device_of, value):
        buf[me] = value

        def copy(to_index, from_index):
            return pltpu.make_async_remote_copy(
                src_ref=buf.at[me],
                dst_ref=buf.at[from_index],
                send_sem=en_send.at[base + to_index],
                recv_sem=en_recv.at[base + from_index],
                device_id=device_of(to_index),
                device_id_type=MESH,
            )

        @pl.loop(1, size)
        def _(k):
            copy((me + k) % size, me).start()

        @pl.loop(1, size)
        def _(k):
            other = (me + k) % size
            copy(other, other).wait_recv()

        total = buf[0]
        for i in range(1, size):
            total = total + buf[i]
        return total, lambda k: copy((me + k) % size, me).wait_send()

    done = []
    value = mine
    plans = (
        (e1, near, lane_pos, 0, lambda i: {"ctx": row * near + i}),
        (e2, n_row, row, near, lambda i: {"ctx": i * near + lane_pos}),
        (e3, n_dp, dp, near + n_row, lambda i: {"dp": i}),
    )
    for buf, size, me, base, device_of in plans:
        if size > 1:
            value, wait = exchange(buf, size, me, base, device_of, value)
            done.append((size, wait))
    energy_ref[...] = value

    for size, wait in done:

        @pl.loop(1, size)
        def _(k, wait=wait):
            wait(k)

    sent(sends)
    sent(relays)

    @pl.when(even | fwd1)
    def _():
        scale_copy().wait_send()

        @pl.loop(0, NG)
        def _(g):
            state_copy(g).wait_send()

    @pl.when(even & bwd1)
    def _():
        @pl.loop(0, NG)
        def _(g):
            up, over = relay_state(g)
            up.wait_send()

            @pl.when(fwd2)
            def _():
                over.wait_send()


def shards(n_dp, n_ctx, near, *args):
    (starts, ends, modes, x, decay, b_in, c_in, gate, skip, gain, q, k, v, lw) = args
    operands = (
        starts,
        ends,
        modes,
        x[0],
        decay[0],
        b_in[0],
        c_in[0],
        gate[0],
        skip,
        gain.reshape(1, H * P_SIZE),
        q[0],
        k[0],
        v[0],
        lw,
    )
    vmem = pl.BlockSpec(memory_space=pltpu.VMEM)
    smem = pl.BlockSpec(memory_space=pltpu.SMEM)
    specs = [vmem] * 8 + [smem] + [vmem] * 5
    n_row = n_ctx // near
    V, D = pltpu.VMEM, pltpu.SemaphoreType.DMA
    ratio = AQ // AK
    scratch = [
        V((2 * REACH + 1, TOK, AK * AD), bf16),
        V((2 * REACH + 1, TOK, AK * AD), bf16),
        V((NG, N, GW), bf16),
        V((NG, N, GW), bf16),
        V((NG, 1, GW), f32),
        V((NG, N, GW), bf16),
        V((NG, N, GW), f32),
        V((NG, 1, GW), f32),
        V((NG, 1, GW), f32),
        V((NG, TOK, GW), f32),
        V((NG, TOK, GW), f32),
        V((TOK, WIN), f32),
        V((TOK, TOK), f32),
        V((TOK, TOK), f32),
        V((TOK, TOK), f32),
        V((8, TOK), f32),
        V((NG, TOK, TOK), f32),
        V((H, TOK), f32),
        V((AK, ratio * TOK, AD), f32),
        V((AK, ratio * TOK, AD), f32),
        V((AK, ratio * TOK, AD), f32),
        V((2, TOK, TOK), f32),
        V((near, 8, TOK), f32),
        V((n_row, 8, TOK), f32),
        V((n_dp, 8, TOK), f32),
        D((6, 2)),
        D((7, 2)),
        D((NG,)),
        D((NG,)),
        D((NG,)),
        D,
        D,
        D((NG,)),
        D((NG,)),
        D((near + n_row + n_dp,)),
        D((near + n_row + n_dp,)),
    ]
    mamba, attn, energy = pl.pallas_call(
        functools.partial(body, n_dp, n_ctx, near),
        out_shape=(
            jax.ShapeDtypeStruct((TOK, H * P_SIZE), bf16),
            jax.ShapeDtypeStruct((TOK, AQ * AD), bf16),
            jax.ShapeDtypeStruct((8, TOK), f32),
        ),
        in_specs=specs,
        out_specs=(vmem, vmem, vmem),
        scratch_shapes=scratch,
        compiler_params=pltpu.CompilerParams(
            collective_id=0, has_side_effects=True, vmem_limit_bytes=60 * 1024 * 1024
        ),
        name="mixers",
    )(*operands)
    return mamba[None], attn[None], energy[:2, :2]


def solution(mesh):
    placed = (
        P("dp", None),
        P("dp", None),
        P("dp", None),
        P("dp", "ctx", None),
        P("dp", None, "ctx"),
        P("dp", "ctx", None),
        P("dp", "ctx", None),
        P("dp", "ctx", None),
        P(),
        P(),
        P("dp", "ctx", None),
        P("dp", "ctx", None),
        P("dp", "ctx", None),
        P("dp", "ctx"),
    )
    n_dp, n_ctx = mesh.shape["dp"], mesh.shape["ctx"]
    return jax.shard_map(
        functools.partial(shards, n_dp, n_ctx, min(16, n_ctx)),
        mesh=mesh,
        in_specs=placed,
        out_specs=(P("dp", "ctx", None), P("dp", "ctx", None), P()),
        check_vma=False,
    )
```

time: 786 us -> 76.7 us (0.10)
  the two profiles are of different devices: /device:TPU:1 before, /device:TPU:8 now
where the time goes in v1:
time: 76.7 us; the launch traced here: 76.6 us
  Pallas kernels  71.4 us (93%)
  local copies, waits for them, and re-layouts  4.59 us (6%)
    pallas_call x1, Pallas kernels, shards(): pl.pallas_call(functools.partial(body, n_dp, n_ctx, near), out_shape=(jax...  71.4 us
    unnamed x4, local copies, waits for them, and re-layouts  3.35 us

profile of v1, /device:TPU:8, one launch (start us, length us, event | category | flops | bytes accessed | tf_op | source)
XLA Modules:
  0.0 76.6 jit_solution(4844738915931968041)
XLA Ops:
  0.6 71.4 %mixers.1 = (bf16[128,4096]{1,0:T(8,128)(2,1)}, bf16[128,4096]{1,0:T(8,128)(2,1)}, f32[8,128]{1,0:T(8,128)}) custom-call(s32[1,64]{1,0:T(1,128)} %starts_ref.1, s32[1,64]{1,0:T(1,128)} %ends_ref.1, s32[1,64]{1,0:T(1,128)} %modes_ref.1, bf16[128,4096]{1,0:T(8,128)(2,1)} %bitcast.13, f32[64,128]{1,0:T(8,128)} %bitcast.20, bf16[128,512]{1,0:T(8,128)(2,1)} %bitcast.18, ...), custom_call_target="tpu_custom_call" | custom-call | tf_op jit(solution)/shard_map/mixers/pallas_call | solution.py:596
  72.0 1.2 %slice.3 = f32[2,2]{1,0:T(2,128)} slice(f32[8,128]{1,0:T(8,128)} %get-tuple-element.8), slice={[0:2], [0:2]} | slice | bytes 32 | tf_op jit(solution)/shard_map/slice | solution.py:611
  73.2 0.0 copy-start
  73.2 2.4 %copy.19 = bf16[1,128,4096]{2,1,0:T(8,128)(2,1)} copy(bf16[1,128,4096]{2,1,0:T(8,128)(2,1)} %bitcast.12) | data formatting | bytes 2097152
  75.6 0.0 copy-done
  75.6 1.0 %copy.20 = bf16[1,128,4096]{2,1,0:T(8,128)(2,1)} copy(bf16[1,128,4096]{2,1,0:T(8,128)(2,1)S(1)} %bitcast.11) | data formatting | bytes 2097152
Async XLA Ops:
  73.2 2.4 %copy-start = (bf16[128,4096]{1,0:T(8,128)(2,1)S(1)}, bf16[128,4096]{1,0:T(8,128)(2,1)}, u32[]{:S(2)}) copy-start(bf16[128,4096]{1,0:T(8,128)(2,1)} %get-tuple-element.7) | copy-start | bytes 3145732

commit v2 on v1

--- a/solution.py
+++ b/solution.py
@@ -47,20 +47,25 @@
     starts_ref,
     ends_ref,
     modes_ref,
-    x_ref,
+    x_hbm,
     decay_ref,
-    b_ref,
-    c_ref,
-    gate_ref,
+    b_hbm,
+    c_hbm,
+    gate_hbm,
     skip_ref,
     gain_ref,
-    q_ref,
-    k_ref,
-    v_ref,
+    q_hbm,
+    k_hbm,
+    v_hbm,
     lw_ref,
     mamba_ref,
     attn_ref,
     energy_ref,
+    x_ref,
+    b_ref,
+    c_ref,
+    gate_ref,
+    q_ref,
     kbuf,
     vbuf,
     abuf,
@@ -85,7 +90,6 @@
     esq,
     e1,
     e2,
-    e3,
     kv_send,
     kv_recv,
     st_send,
@@ -97,6 +101,7 @@
     rel2,
     en_send,
     en_recv,
+    in_sem,
 ):
     b = lax.axis_index("ctx")
     dp = lax.axis_index("dp")
@@ -119,11 +124,14 @@
     def _(k):
         greet({"ctx": row * near + (lane_pos + k) % near})
 
-    for k in range(1, n_row):
-        greet({"ctx": ((row + k) % n_row) * near + lane_pos})
-    for k in range(1, n_dp):
-        greet({"dp": (dp + k) % n_dp})
-    count = near - 1 + n_row - 1 + n_dp - 1
+    columns = n_row * n_dp
+
+    @pl.loop(1, columns)
+    def _(k):
+        i = (dp * n_row + row + k) % columns
+        greet({"dp": i // n_row, "ctx": (i % n_row) * near + lane_pos})
+
+    count = near - 1 + columns - 1
     for d in (-2, -1, 1, 2):
         ok = (b + d >= 0) & (b + d < n_ctx)
 
@@ -132,6 +140,23 @@
             greet({"ctx": b + d})
 
         count = count + jnp.where(ok, 1, 0)
+
+    loads = [
+        pltpu.make_async_copy(src, dst, in_sem.at[i])
+        for i, (src, dst) in enumerate(
+            (
+                (x_hbm, x_ref),
+                (b_hbm, b_ref),
+                (c_hbm, c_ref),
+                (k_hbm, kbuf.at[REACH]),
+                (v_hbm, vbuf.at[REACH]),
+                (q_hbm, q_ref),
+                (gate_hbm, gate_ref),
+            )
+        )
+    ]
+    for load in loads:
+        load.start()
 
     st_row = starts_ref[...].astype(f32)
     en_row = ends_ref[...].astype(f32)
@@ -206,8 +231,8 @@
         )
 
     def kv(which_send, from_slot, to_slot, to):
-        k_src = k_ref if from_slot is None else kbuf.at[from_slot]
-        v_src = v_ref if from_slot is None else vbuf.at[from_slot]
+        k_src = k_hbm if from_slot is None else kbuf.at[from_slot]
+        v_src = v_hbm if from_slot is None else vbuf.at[from_slot]
         return (
             remote(k_src, kbuf.at[to_slot], kv_send.at[which_send, 0], kv_recv.at[to_slot, 0], to),
             remote(v_src, vbuf.at[to_slot], kv_send.at[which_send, 1], kv_recv.at[to_slot, 1], to),
@@ -254,6 +279,8 @@
                 copy.wait_recv()
 
     start(sends)
+    for load in loads[:3]:
+        load.wait()
 
     lane = iota((TOK, TOK), 1)
     left = lane < P_SIZE
@@ -358,10 +385,10 @@
             axis=0,
         )
         keys = jnp.concatenate(
-            [(k_ref[:, heads] if i == REACH else kbuf[i, :, heads]) for i in slots], axis=0
+            [kbuf[i, :, heads] for i in slots], axis=0
         )
         values = jnp.concatenate(
-            [(v_ref[:, heads] if i == REACH else vbuf[i, :, heads]) for i in slots], axis=0
+            [vbuf[i, :, heads] for i in slots], axis=0
         )
         masks = jnp.concatenate([bias[:, i * TOK : (i + 1) * TOK] for i in slots], axis=1)
         s = dot(q, keys, NT) * scale
@@ -370,6 +397,8 @@
         wide = jnp.concatenate([values, jnp.ones_like(values)], axis=1)
         return s, wide
 
+    for load in loads[3:]:
+        load.wait()
     near_slots, far_slots = (1, 2, 3, 4, 5), (0, 6)
     arrived(2)
     arrived(4)
@@ -425,10 +454,6 @@
             square = square + wide_piece * wide_piece
         esq[1] = esq[1] + square
 
-    @pl.when(odd)
-    def _():
-        pass
-
     @pl.when(even & bwd1)
     def _():
         scale_copy().wait_recv()
@@ -493,14 +518,19 @@
     value = mine
     plans = (
         (e1, near, lane_pos, 0, lambda i: {"ctx": row * near + i}),
-        (e2, n_row, row, near, lambda i: {"ctx": i * near + lane_pos}),
-        (e3, n_dp, dp, near + n_row, lambda i: {"dp": i}),
+        (
+            e2,
+            n_row * n_dp,
+            dp * n_row + row,
+            near,
+            lambda i: {"dp": i // n_row, "ctx": (i % n_row) * near + lane_pos},
+        ),
     )
     for buf, size, me, base, device_of in plans:
         if size > 1:
             value, wait = exchange(buf, size, me, base, device_of, value)
             done.append((size, wait))
-    energy_ref[...] = value
+    energy_ref[...] = value[:2, :2]
 
     for size, wait in done:
 
@@ -551,11 +581,17 @@
     )
     vmem = pl.BlockSpec(memory_space=pltpu.VMEM)
     smem = pl.BlockSpec(memory_space=pltpu.SMEM)
-    specs = [vmem] * 8 + [smem] + [vmem] * 5
+    hbm = pl.BlockSpec(memory_space=pl.ANY)
+    specs = [vmem] * 3 + [hbm, vmem, hbm, hbm, hbm, smem, vmem, hbm, hbm, hbm, vmem]
     n_row = n_ctx // near
     V, D = pltpu.VMEM, pltpu.SemaphoreType.DMA
     ratio = AQ // AK
     scratch = [
+        V((TOK, H * P_SIZE), bf16),
+        V((TOK, NG * N), bf16),
+        V((TOK, NG * N), bf16),
+        V((TOK, H * P_SIZE), bf16),
+        V((TOK, AQ * AD), bf16),
         V((2 * REACH + 1, TOK, AK * AD), bf16),
         V((2 * REACH + 1, TOK, AK * AD), bf16),
         V((NG, N, GW), bf16),
@@ -579,8 +615,7 @@
         V((AK, ratio * TOK, AD), f32),
         V((2, TOK, TOK), f32),
         V((near, 8, TOK), f32),
-        V((n_row, 8, TOK), f32),
-        V((n_dp, 8, TOK), f32),
+        V((n_row * n_dp, 8, TOK), f32),
         D((6, 2)),
         D((7, 2)),
         D((NG,)),
@@ -590,15 +625,16 @@
         D,
         D((NG,)),
         D((NG,)),
-        D((near + n_row + n_dp,)),
-        D((near + n_row + n_dp,)),
+        D((near + n_row * n_dp,)),
+        D((near + n_row * n_dp,)),
+        D((7,)),
     ]
     mamba, attn, energy = pl.pallas_call(
         functools.partial(body, n_dp, n_ctx, near),
         out_shape=(
-            jax.ShapeDtypeStruct((TOK, H * P_SIZE), bf16),
-            jax.ShapeDtypeStruct((TOK, AQ * AD), bf16),
-            jax.ShapeDtypeStruct((8, TOK), f32),
+            pltpu.VMEM((TOK, H * P_SIZE), bf16),
+            pltpu.VMEM((TOK, AQ * AD), bf16),
+            jax.ShapeDtypeStruct((2, 2), f32),
         ),
         in_specs=specs,
         out_specs=(vmem, vmem, vmem),
@@ -608,7 +644,7 @@
         ),
         name="mixers",
     )(*operands)
-    return mamba[None], attn[None], energy[:2, :2]
+    return mamba[None], attn[None], energy
 
 
 def solution(mesh):

time: 76.7 us -> 71.5 us (0.932)
  the two profiles are of different devices: /device:TPU:8 before, /device:TPU:1 now
where the time goes in v2:
time: 71.5 us; the launch traced here: 71.4 us
  Pallas kernels  68.2 us (95%)
  local copies, waits for them, and re-layouts  2.51 us (4%)
    pallas_call x1, Pallas kernels, shards(): pl.pallas_call(functools.partial(body, n_dp, n_ctx, near), out_shape=(plt...  68.2 us
    unnamed x5, local copies, waits for them, and re-layouts  2.51 us

profile of v2, /device:TPU:1, one launch (start us, length us, event | category | flops | bytes accessed | tf_op | source)
XLA Modules:
  0.0 71.4 jit_solution(17420071215718790742)
XLA Ops:
  0.6 68.2 %mixers.1 = (bf16[128,4096]{1,0:T(8,128)(2,1)S(1)}, bf16[128,4096]{1,0:T(8,128)(2,1)S(1)}, f32[2,2]{1,0:T(2,128)}) custom-call(s32[1,64]{1,0:T(1,128)} %starts_ref.1, s32[1,64]{1,0:T(1,128)} %ends_ref.1, s32[1,64]{1,0:T(1,128)} %modes_ref.1, bf16[128,4096]{1,0:T(8,128)(2,1)} %bitcast.13, f32[64,128]{1,0:T(8,128)} %bitcast.20, bf16[128,512]{1,0:T(8,128)(2,1)} %bitcast.18, ...), custom_call_target="tpu_custom_call" | custom-call | tf_op jit(solution)/shard_map/mixers/pallas_call | solution.py:632
  68.8 1.0 %copy.20 = bf16[1,128,4096]{2,1,0:T(8,128)(2,1)} copy(bf16[1,128,4096]{2,1,0:T(8,128)(2,1)S(1)} %bitcast.12) | data formatting | bytes 2097152
  69.8 0.0 copy-start
  69.8 1.0 %copy.21 = bf16[1,128,4096]{2,1,0:T(8,128)(2,1)} copy(bf16[1,128,4096]{2,1,0:T(8,128)(2,1)S(1)} %bitcast.11) | data formatting | bytes 2097152
  70.8 0.0 copy-done
  70.8 0.6 copy.22
Async XLA Ops:
  69.8 1.0 %copy-start = (f32[2,2]{1,0:T(2,128)S(1)}, f32[2,2]{1,0:T(2,128)}, u32[]{:S(2)}) copy-start(f32[2,2]{1,0:T(2,128)} %get-tuple-element.17) | copy-start | bytes 52

commit v3 on v2

--- a/solution.py
+++ b/solution.py
@@ -15,6 +15,7 @@
 AQ = 32
 AK = 8
 AD = 128
+HALF = 64
 REACH = 3
 TOK = 128
 WIN = (2 * REACH + 1) * TOK
@@ -70,6 +71,11 @@
     vbuf,
     abuf,
     bbuf,
+    hbuf,
+    hsend,
+    chead,
+    wtail,
+    reach,
     sbuf,
     ebuf,
     ewide,
@@ -98,7 +104,10 @@
     s_send,
     s_recv,
     rel1,
-    rel2,
+    h_send,
+    h_recv,
+    ch_send,
+    ch_recv,
     en_send,
     en_recv,
     in_sem,
@@ -120,26 +129,26 @@
     def greet(device):
         pl.semaphore_signal(barrier, inc=1, device_id=device, device_id_type=MESH)
 
+    columns = n_row * n_dp
+    count = near - 1 + columns - 1
+    for d in (-2, -1, 1, 2):
+        ok = (b + d >= 0) & (b + d < n_ctx)
+
+        @pl.when(ok)
+        def _(d=d):
+            greet({"ctx": b + d})
+
+        count = count + jnp.where(ok, 1, 0)
+
     @pl.loop(1, near)
     def _(k):
         greet({"ctx": row * near + (lane_pos + k) % near})
-
-    columns = n_row * n_dp
 
     @pl.loop(1, columns)
     def _(k):
         i = (dp * n_row + row + k) % columns
         greet({"dp": i // n_row, "ctx": (i % n_row) * near + lane_pos})
 
-    count = near - 1 + columns - 1
-    for d in (-2, -1, 1, 2):
-        ok = (b + d >= 0) & (b + d < n_ctx)
-
-        @pl.when(ok)
-        def _(d=d):
-            greet({"ctx": b + d})
-
-        count = count + jnp.where(ok, 1, 0)
 
     loads = [
         pltpu.make_async_copy(src, dst, in_sem.at[i])
@@ -157,6 +166,75 @@
     ]
     for load in loads:
         load.start()
+
+    pl.semaphore_wait(barrier, count)
+
+    def remote(src, dst, send, recv, to):
+        return pltpu.make_async_remote_copy(
+            src_ref=src,
+            dst_ref=dst,
+            send_sem=send,
+            recv_sem=recv,
+            device_id=peer(to),
+            device_id_type=MESH,
+        )
+
+    def kv(which_send, from_slot, to_slot, to):
+        k_src = k_hbm if from_slot is None else kbuf.at[from_slot]
+        v_src = v_hbm if from_slot is None else vbuf.at[from_slot]
+        return (
+            remote(k_src, kbuf.at[to_slot], kv_send.at[which_send, 0], kv_recv.at[to_slot, 0], to),
+            remote(v_src, vbuf.at[to_slot], kv_send.at[which_send, 1], kv_recv.at[to_slot, 1], to),
+        )
+
+    fwd2, bwd2 = b + 2 < n_ctx, b - 2 >= 0
+    fwd1, bwd1 = b + 1 < n_ctx, b - 1 >= 0
+    has_r2, has_l2 = bwd2, fwd2
+    sends = [
+        (fwd2, lambda: kv(0, None, 1, b + 2)),
+        (bwd2, lambda: kv(1, None, 5, b - 2)),
+        (even, lambda: kv(2, None, 2, b + 1)),
+        (odd, lambda: kv(2, None, 4, b - 1)),
+    ]
+    relays = [
+        (has_r2 & even, lambda: kv(3, 1, 0, b + 1)),
+        (has_r2 & odd, lambda: kv(3, 1, 2, b - 1)),
+        (has_l2 & even, lambda: kv(4, 5, 4, b + 1)),
+        (has_l2 & odd, lambda: kv(4, 5, 6, b - 1)),
+        (has_l2 & even & bwd1, lambda: kv(5, 5, 6, b - 1)),
+    ]
+    far = [(even & bwd1 & fwd2, lambda: kv(6, 2, 0, b + 2))]
+
+    def start(plan):
+        for when, make in plan:
+
+            @pl.when(when)
+            def _(make=make):
+                for copy in make():
+                    copy.start()
+
+    def sent(plan):
+        for when, make in plan:
+
+            @pl.when(when)
+            def _(make=make):
+                for copy in make():
+                    copy.wait_send()
+
+    def arrived(slot):
+        @pl.when((b - REACH + slot >= 0) & (b - REACH + slot < n_ctx))
+        def _():
+            for copy in kv(0, None, slot, b):
+                copy.wait_recv()
+
+    start(sends)
+
+    def head_copy():
+        return remote(c_hbm.at[:HALF], chead, ch_send, ch_recv, b - 2)
+
+    @pl.when(even & bwd2)
+    def _():
+        head_copy().start()
 
     st_row = starts_ref[...].astype(f32)
     en_row = ends_ref[...].astype(f32)
@@ -189,6 +267,15 @@
     )
     carried = jnp.where(begin_col < first_f, 1.0, 0.0)
     carm[...] = jnp.broadcast_to(carried, (TOK, TOK))
+
+    def goes_on(base):
+        end = jnp.where((st_row < base) & (base <= en_row), en_row, 0.0)
+        return jnp.sum(jnp.where(end > base + float(2 * TOK + HALF), 1.0, 0.0), axis=1, keepdims=True)
+
+    chip_first = (first - core * TOK).astype(f32)
+    rows_out = goes_on(first_f + float(TOK))
+    rows_in = goes_on(chip_first)
+    rows_before = goes_on(chip_first - float(2 * TOK))
     own_pos = key_pos[:, own]
     own_member = jnp.where((st_col <= own_pos) & (own_pos < en_col), 1.0, 0.0)
     mode_row = jnp.sum(own_member * mo_col, axis=0, keepdims=True)
@@ -214,71 +301,14 @@
         abuf[...] = jnp.zeros_like(abuf)
         sbuf[...] = jnp.zeros_like(sbuf)
 
+    @pl.when(b < 4)
+    def _():
+        hbuf[...] = jnp.zeros_like(hbuf)
+
     @pl.when(b < 3)
     def _():
         bbuf[...] = jnp.zeros_like(bbuf)
 
-    pl.semaphore_wait(barrier, count)
-
-    def remote(src, dst, send, recv, to):
-        return pltpu.make_async_remote_copy(
-            src_ref=src,
-            dst_ref=dst,
-            send_sem=send,
-            recv_sem=recv,
-            device_id=peer(to),
-            device_id_type=MESH,
-        )
-
-    def kv(which_send, from_slot, to_slot, to):
-        k_src = k_hbm if from_slot is None else kbuf.at[from_slot]
-        v_src = v_hbm if from_slot is None else vbuf.at[from_slot]
-        return (
-            remote(k_src, kbuf.at[to_slot], kv_send.at[which_send, 0], kv_recv.at[to_slot, 0], to),
-            remote(v_src, vbuf.at[to_slot], kv_send.at[which_send, 1], kv_recv.at[to_slot, 1], to),
-        )
-
-    fwd2, bwd2 = b + 2 < n_ctx, b - 2 >= 0
-    fwd1, bwd1 = b + 1 < n_ctx, b - 1 >= 0
-    has_r2, has_l2 = bwd2, fwd2
-    sends = [
-        (fwd2, lambda: kv(0, None, 1, b + 2)),
-        (bwd2, lambda: kv(1, None, 5, b - 2)),
-        (even, lambda: kv(2, None, 2, b + 1)),
-        (odd, lambda: kv(2, None, 4, b - 1)),
-    ]
-    relays = [
-        (has_r2 & even, lambda: kv(3, 1, 0, b + 1)),
-        (has_r2 & odd, lambda: kv(3, 1, 2, b - 1)),
-        (has_l2 & even, lambda: kv(4, 5, 4, b + 1)),
-        (has_l2 & odd, lambda: kv(4, 5, 6, b - 1)),
-        (has_r2 & odd & fwd1, lambda: kv(5, 1, 0, b + 1)),
-        (has_l2 & even & bwd1, lambda: kv(5, 5, 6, b - 1)),
-    ]
-
-    def start(plan):
-        for when, make in plan:
-
-            @pl.when(when)
-            def _(make=make):
-                for copy in make():
-                    copy.start()
-
-    def sent(plan):
-        for when, make in plan:
-
-            @pl.when(when)
-            def _(make=make):
-                for copy in make():
-                    copy.wait_send()
-
-    def arrived(slot):
-        @pl.when((b - REACH + slot >= 0) & (b - REACH + slot < n_ctx))
-        def _():
-            for copy in kv(0, None, slot, b):
-                copy.wait_recv()
-
-    start(sends)
     for load in loads[:3]:
         load.wait()
 
@@ -307,6 +337,7 @@
             lanes = pl.ds(pl.multiple_of(g * GW + pair * TOK, TOK), TOK)
             parts.append((x_ref[:, lanes].astype(f32) * tail).astype(bf16))
         weighted = jnp.concatenate(parts, axis=1)
+        wtail[g] = weighted[HALF:, :]
         b_grp = b_ref[:, pl.ds(pl.multiple_of(g * N, N), N)]
         e = dot(b_grp, weighted, TN)
         ewide[g] = e
@@ -332,7 +363,12 @@
 
     def combine(g):
         state_copy(g).wait_recv()
-        ebuf[g] = (ewide[g] + tbuf[g] * abuf[g].astype(f32)).astype(bf16)
+        state = ewide[g] + tbuf[g] * abuf[g].astype(f32)
+        top = wtail[g].astype(f32)
+        b_rows = b_ref[HALF:, g * N : (g + 1) * N].astype(f32)
+        low = jnp.concatenate([b_rows, top[:, N:]], axis=1)
+        rows = jnp.concatenate([top, low], axis=0)
+        ebuf[g] = jnp.where(rows_out > 0.5, rows, state).astype(bf16)
 
         @pl.when(fwd1)
         def _():
@@ -340,8 +376,8 @@
 
     @pl.when(odd)
     def _():
-        combine(0)
-        combine(1)
+        for g in range(NG):
+            combine(g)
 
     @pl.loop(0, NG)
     def _(g):
@@ -366,12 +402,6 @@
     arrived(1)
     arrived(5)
     start(relays)
-
-    @pl.when(odd)
-    def _():
-        combine(2)
-        combine(3)
-
     ratio = AQ // AK
     scale = AD ** (-0.5) * math.log2(math.e)
 
@@ -401,11 +431,12 @@
         load.wait()
     near_slots, far_slots = (1, 2, 3, 4, 5), (0, 6)
     arrived(2)
+    start(far)
     arrived(4)
 
     def relay_state(g):
         up = remote(abuf.at[g], bbuf.at[g], rel1.at[g], b_recv.at[g], b + 1)
-        over = remote(abuf.at[g], bbuf.at[g], rel2.at[g], b_recv.at[g], b + 2)
+        over = remote(hsend.at[g], hbuf.at[g], h_send.at[g], h_recv.at[g], b + 2)
         return up, over
 
     def pass_on(g):
@@ -414,11 +445,21 @@
             state_copy(g).wait_recv()
             up, over = relay_state(g)
 
+            up.start()
+
             @pl.when(fwd2)
             def _():
+                raw = abuf[g]
+                c_rows = chead[:, pl.ds(pl.multiple_of(g * N, N), N)]
+                seen = dot(c_rows, raw)
+                kept = jnp.where(rows_in > 0.5, raw[:HALF].astype(f32), seen)
+                hsend[g, :, :GW] = kept.astype(bf16)
+                hsend[g, :, GW:] = raw[HALF:, :N]
                 over.start()
 
-            up.start()
+    @pl.when(even & fwd2)
+    def _():
+        remote(chead, chead, ch_send, ch_recv, b).wait_recv()
 
     @pl.loop(0, NG)
     def _(g):
@@ -458,14 +499,40 @@
     def _():
         scale_copy().wait_recv()
 
+    def unpack(raw):
+        built = dot(raw[HALF:, :N], raw[:HALF, :], TN)
+        return jnp.where(rows_in > 0.5, built, raw.astype(f32)).astype(bf16)
+
     @pl.loop(0, NG)
     def _(g):
-        @pl.when(b >= 3)
+        c_grp = c_ref[:, pl.ds(pl.multiple_of(g * N, N), N)]
+
+        @pl.when(even)
         def _():
-            remote(bbuf.at[g], bbuf.at[g], rel1.at[g], b_recv.at[g], b).wait_recv()
-
-        c_grp = c_ref[:, pl.ds(pl.multiple_of(g * N, N), N)]
-        reached = dot(c_grp, abuf[g]) + dot(c_grp, bbuf[g]) * sbuf[g]
+            near_part = dot(c_grp, unpack(abuf[g]))
+
+            @pl.when(b >= 4)
+            def _():
+                remote(hbuf.at[g], hbuf.at[g], h_send.at[g], h_recv.at[g], b).wait_recv()
+
+            half = hbuf[g, :, :GW]
+            built = dot(hbuf[g, :, GW:], half, TN).astype(bf16)
+            seen = half.astype(f32)
+            seen = jnp.concatenate([seen, jnp.zeros_like(seen)], axis=0)
+            far_part = jnp.where(rows_before > 0.5, dot(c_grp, built), seen)
+            reach[...] = near_part + far_part * sbuf[g]
+
+        @pl.when(odd)
+        def _():
+            near_part = dot(c_grp, abuf[g])
+
+            @pl.when(b >= 3)
+            def _():
+                remote(bbuf.at[g], bbuf.at[g], rel1.at[g], b_recv.at[g], b).wait_recv()
+
+            reach[...] = near_part + dot(c_grp, unpack(bbuf[g])) * sbuf[g]
+
+        reached = reach[...]
         lanes = pl.ds(pl.multiple_of(g * GW, GW), GW)
         result = res[g] + reached * fx[g]
         z = gate_ref[:, lanes].astype(f32)
@@ -500,8 +567,7 @@
                 device_id_type=MESH,
             )
 
-        @pl.loop(1, size)
-        def _(k):
+        for k in sorted(range(1, size), key=lambda k: -min(k, size - k)):
             copy((me + k) % size, me).start()
 
         @pl.loop(1, size)
@@ -540,6 +606,7 @@
 
     sent(sends)
     sent(relays)
+    sent(far)
 
     @pl.when(even | fwd1)
     def _():
@@ -548,6 +615,10 @@
         @pl.loop(0, NG)
         def _(g):
             state_copy(g).wait_send()
+
+    @pl.when(even & bwd2)
+    def _():
+        head_copy().wait_send()
 
     @pl.when(even & bwd1)
     def _():
@@ -559,6 +630,15 @@
             @pl.when(fwd2)
             def _():
                 over.wait_send()
+
+
+def put_out(*refs):
+    sem = refs[-1]
+    copies = [pltpu.make_async_copy(refs[i], refs[3 + i], sem.at[i]) for i in range(3)]
+    for copy in copies:
+        copy.start()
+    for copy in copies:
+        copy.wait()
 
 
 def shards(n_dp, n_ctx, near, *args):
@@ -596,6 +676,11 @@
         V((2 * REACH + 1, TOK, AK * AD), bf16),
         V((NG, N, GW), bf16),
         V((NG, N, GW), bf16),
+        V((NG, HALF, GW + N), bf16),
+        V((NG, HALF, GW + N), bf16),
+        V((HALF, NG * N), bf16),
+        V((NG, HALF, GW), bf16),
+        V((TOK, GW), f32),
         V((NG, 1, GW), f32),
         V((NG, N, GW), bf16),
         V((NG, N, GW), f32),
@@ -616,7 +701,7 @@
         V((2, TOK, TOK), f32),
         V((near, 8, TOK), f32),
         V((n_row * n_dp, 8, TOK), f32),
-        D((6, 2)),
+        D((7, 2)),
         D((7, 2)),
         D((NG,)),
         D((NG,)),
@@ -625,6 +710,9 @@
         D,
         D((NG,)),
         D((NG,)),
+        D((NG,)),
+        D,
+        D,
         D((near + n_row * n_dp,)),
         D((near + n_row * n_dp,)),
         D((7,)),
@@ -634,7 +722,7 @@
         out_shape=(
             pltpu.VMEM((TOK, H * P_SIZE), bf16),
             pltpu.VMEM((TOK, AQ * AD), bf16),
-            jax.ShapeDtypeStruct((2, 2), f32),
+            pltpu.VMEM((2, 2), f32),
         ),
         in_specs=specs,
         out_specs=(vmem, vmem, vmem),
@@ -644,6 +732,15 @@
         ),
         name="mixers",
     )(*operands)
+    results = (mamba, attn, energy)
+    mamba, attn, energy = pl.pallas_call(
+        put_out,
+        out_shape=tuple(jax.ShapeDtypeStruct(r.shape, r.dtype) for r in results),
+        in_specs=[vmem] * 3,
+        out_specs=(hbm,) * 3,
+        scratch_shapes=[D((3,))],
+        name="put_out",
+    )(*[pltpu.with_memory_space_constraint(r, pltpu.VMEM) for r in results])
     return mamba[None], attn[None], energy
 
 

time: 71.5 us -> 66.5 us (0.930)
  local copies, waits for them, and re-layouts: 2.51 us -> 0 us
  Pallas kernels: 68.2 us -> 65.7 us
    pallas_call x1, Pallas kernels: 68.2 us -> 64.3 us  [shards(): pl.pallas_call(functools.partial(body, n_dp, n_ctx, near), out_shape=(plt...]
    unnamed x5 -> x0, local copies, waits for them, and re-layouts: 2.51 us -> none
    pallas_call x0 -> x1, Pallas kernels: none -> 1.35 us  [shards(): pl.pallas_call(put_out, out_shape=tuple((jax.ShapeDtypeStruct(r.shape, r....]
where the time goes in v3:
time: 66.5 us; the launch traced here: 66.3 us
  Pallas kernels  65.7 us (99%)
    pallas_call x1, Pallas kernels, shards(): pl.pallas_call(functools.partial(body, n_dp, n_ctx, near), out_shape=(plt...  64.3 us
    pallas_call x1, Pallas kernels, shards(): pl.pallas_call(put_out, out_shape=tuple((jax.ShapeDtypeStruct(r.shape, r....  1.35 us

profile of v3, /device:TPU:1, one launch (start us, length us, event | category | flops | bytes accessed | tf_op | source)
XLA Modules:
  0.0 66.3 jit_solution(8179313621645479644)
XLA Ops:
  0.6 64.3 %mixers.1 = (bf16[128,4096]{1,0:T(8,128)(2,1)S(1)}, bf16[128,4096]{1,0:T(8,128)(2,1)S(1)}, f32[2,2]{1,0:T(2,128)S(1)}) custom-call(s32[1,64]{1,0:T(1,128)} %starts_ref.1, s32[1,64]{1,0:T(1,128)} %ends_ref.1, s32[1,64]{1,0:T(1,128)} %modes_ref.1, bf16[128,4096]{1,0:T(8,128)(2,1)} %bitcast.11, f32[64,128]{1,0:T(8,128)} %bitcast.18, bf16[128,512]{1,0:T(8,128)(2,1)} %bitcast.16, ...), custom_call_target="tpu_custom_call" | custom-call | tf_op jit(solution)/shard_map/mixers/pallas_call | solution.py:720
  65.0 1.3 %put_out.1 = (bf16[128,4096]{1,0:T(8,128)(2,1)}, bf16[128,4096]{1,0:T(8,128)(2,1)}, f32[2,2]{1,0:T(2,128)}) custom-call(bf16[128,4096]{1,0:T(8,128)(2,1)S(1)} %get-tuple-element.9.refs_0_, bf16[128,4096]{1,0:T(8,128)(2,1)S(1)} %get-tuple-element.10.refs_1_, f32[2,2]{1,0:T(2,128)S(1)} %get-tuple-element.11.refs_2_), custom_call_target="tpu_custom_call" | custom-call | tf_op jit(solution)/shard_map/put_out/pallas_call | solution.py:736

commit v4 on v3

--- a/solution.py
+++ b/solution.py
@@ -76,6 +76,7 @@
     chead,
     wtail,
     reach,
+    lift,
     sbuf,
     ebuf,
     ewide,
@@ -107,6 +108,7 @@
     h_send,
     h_recv,
     ch_send,
+    chn_send,
     ch_recv,
     en_send,
     en_recv,
@@ -203,7 +205,14 @@
         (has_l2 & odd, lambda: kv(4, 5, 6, b - 1)),
         (has_l2 & even & bwd1, lambda: kv(5, 5, 6, b - 1)),
     ]
-    far = [(even & bwd1 & fwd2, lambda: kv(6, 2, 0, b + 2))]
+
+    def half_kv(to):
+        return tuple(
+            remote(buf.at[2, HALF:], buf.at[0, HALF:], kv_send.at[6, i], kv_recv.at[0, i], to)
+            for i, buf in enumerate((kbuf, vbuf))
+        )
+
+    far = [(even & bwd1 & fwd2, lambda: half_kv(b + 2))]
 
     def start(plan):
         for when, make in plan:
@@ -232,8 +241,12 @@
     def head_copy():
         return remote(c_hbm.at[:HALF], chead, ch_send, ch_recv, b - 2)
 
+    def near_head_copy():
+        return remote(c_hbm.at[:HALF], chead, chn_send, ch_recv, b - 1)
+
     @pl.when(even & bwd2)
     def _():
+        near_head_copy().start()
         head_copy().start()
 
     st_row = starts_ref[...].astype(f32)
@@ -272,7 +285,13 @@
         end = jnp.where((st_row < base) & (base <= en_row), en_row, 0.0)
         return jnp.sum(jnp.where(end > base + float(2 * TOK + HALF), 1.0, 0.0), axis=1, keepdims=True)
 
+    def ends_soon(base):
+        end = jnp.where((st_row < base) & (base <= en_row), en_row, 0.0)
+        return jnp.sum(end, axis=1, keepdims=True) <= base + float(HALF)
+
     chip_first = (first - core * TOK).astype(f32)
+    short_out = jnp.where(ends_soon(first_f + float(TOK)), 1.0, 0.0)
+    short_in = jnp.where(ends_soon(chip_first), 1.0, 0.0)
     rows_out = goes_on(first_f + float(TOK))
     rows_in = goes_on(chip_first)
     rows_before = goes_on(chip_first - float(2 * TOK))
@@ -368,7 +387,14 @@
         b_rows = b_ref[HALF:, g * N : (g + 1) * N].astype(f32)
         low = jnp.concatenate([b_rows, top[:, N:]], axis=1)
         rows = jnp.concatenate([top, low], axis=0)
-        ebuf[g] = jnp.where(rows_out > 0.5, rows, state).astype(bf16)
+        kept = jnp.where(rows_out > 0.5, rows, state)
+        seen = dot(chead[:, g * N : (g + 1) * N], state.astype(bf16))
+        if g == NG - 2:
+            low = kbuf[1, :HALF, :].astype(f32)
+        if g == NG - 1:
+            low = vbuf[1, :HALF, :].astype(f32)
+        brief = jnp.concatenate([seen, low], axis=0)
+        ebuf[g] = jnp.where(short_out > 0.5, brief, kept).astype(bf16)
 
         @pl.when(fwd1)
         def _():
@@ -376,11 +402,24 @@
 
     @pl.when(odd)
     def _():
-        for g in range(NG):
+        @pl.when(fwd1)
+        def _():
+            remote(chead, chead, ch_send, ch_recv, b).wait_recv()
+
+        @pl.when(b == n_ctx - 1)
+        def _():
+            chead[...] = jnp.zeros_like(chead)
+
+        for g in range(NG - 2):
             combine(g)
+
+    for load in loads[3:]:
+        load.wait()
 
     @pl.loop(0, NG)
     def _(g):
+        z = gate_ref[:, pl.ds(pl.multiple_of(g * GW, GW), GW)].astype(f32)
+        lift[g] = z / (1.0 + jnp.exp(-z))
         lanes_n = pl.ds(pl.multiple_of(g * N, N), N)
         both_docs = dot(c_ref[:, lanes_n], b_ref[:, lanes_n], NT) * mmask[...]
         cols = runc[g]
@@ -399,11 +438,14 @@
             skip = jnp.where(left, skip_ref[h0], skip_ref[h0 + 1])
             res[g, :, at] = inner + skip * xp.astype(f32)
 
-    arrived(1)
-    arrived(5)
-    start(relays)
+
     ratio = AQ // AK
     scale = AD ** (-0.5) * math.log2(math.e)
+
+    def block_lanes(i):
+        if isinstance(i, int):
+            return slice(i * TOK, (i + 1) * TOK)
+        return pl.ds(pl.multiple_of(i * TOK, TOK), TOK)
 
     def attend(j, slots):
         heads = pl.ds(pl.multiple_of(j * AD, AD), AD)
@@ -420,24 +462,79 @@
         values = jnp.concatenate(
             [vbuf[i, :, heads] for i in slots], axis=0
         )
-        masks = jnp.concatenate([bias[:, i * TOK : (i + 1) * TOK] for i in slots], axis=1)
+        masks = jnp.concatenate([bias[:, block_lanes(i)] for i in slots], axis=1)
         s = dot(q, keys, NT) * scale
         s = s.reshape(ratio, TOK, len(slots) * TOK) + masks[None]
         s = s.reshape(ratio * TOK, len(slots) * TOK)
         wide = jnp.concatenate([values, jnp.ones_like(values)], axis=1)
         return s, wide
 
-    for load in loads[3:]:
-        load.wait()
-    near_slots, far_slots = (1, 2, 3, 4, 5), (0, 6)
-    arrived(2)
+    beside = jnp.where(even, REACH + 1, REACH - 1)
+    chip_slots = (REACH, beside)
+    far_one = jnp.where(even, 0, 2 * REACH)
+    near_slots = (1, 5, 2 * REACH - beside, 2 * REACH - far_one)
+    far_slots = (far_one,)
+
+    @pl.when(even)
+    def _():
+        arrived(4)
+
+    @pl.when(odd)
+    def _():
+        arrived(2)
+
+    @pl.loop(0, AK)
+    def _(j):
+        s, wide = attend(j, chip_slots)
+        top = jnp.max(s, axis=1, keepdims=True)
+        p = jnp.exp2(s - top).astype(bf16)
+        o = dot(p, wide)
+        acc[j] = o[:, :AD]
+        lsum[j] = o[:, AD:]
+        mtop[j] = jnp.broadcast_to(top, (ratio * TOK, AD))
+
+    def fold(j, slots):
+        s, wide = attend(j, slots)
+        before = mtop[j]
+        top = jnp.maximum(before, jnp.max(s, axis=1, keepdims=True))
+        p = jnp.exp2(s - jnp.concatenate([top] * len(slots), axis=1)).astype(bf16)
+        o = dot(p, wide)
+        fade = jnp.exp2(before - top)
+        return acc[j] * fade + o[:, :AD], lsum[j] * fade + o[:, AD:], top
+
+    arrived(1)
+
+    @pl.when(odd)
+    def _():
+        combine(NG - 2)
+        combine(NG - 1)
+
+    start(relays[:2])
+    arrived(5)
+    start(relays[2:])
+    @pl.when(even)
+    def _():
+        arrived(2)
+
     start(far)
-    arrived(4)
+
+    @pl.when(even)
+    def _():
+        arrived(6)
+
+    @pl.when(odd)
+    def _():
+        arrived(4)
+        arrived(0)
 
     def relay_state(g):
         up = remote(abuf.at[g], bbuf.at[g], rel1.at[g], b_recv.at[g], b + 1)
         over = remote(hsend.at[g], hbuf.at[g], h_send.at[g], h_recv.at[g], b + 2)
         return up, over
+
+    def unpack(raw):
+        built = dot(raw[HALF:, :N], raw[:HALF, :], TN)
+        return jnp.where(rows_in > 0.5, built, raw.astype(f32)).astype(bf16)
 
     def pass_on(g):
         @pl.when(even & bwd1)
@@ -457,36 +554,41 @@
                 hsend[g, :, GW:] = raw[HALF:, :N]
                 over.start()
 
+            c_grp = c_ref[:, pl.ds(pl.multiple_of(g * N, N), N)]
+            raw = abuf[g]
+            upper = raw[:HALF].astype(f32)
+            brief = jnp.concatenate([upper, jnp.zeros_like(upper)], axis=0)
+            got = jnp.where(short_in > 0.5, brief, dot(c_grp, unpack(raw)))
+            res[g] = res[g] + got * fx[g]
+
     @pl.when(even & fwd2)
     def _():
         remote(chead, chead, ch_send, ch_recv, b).wait_recv()
-
-    @pl.loop(0, NG)
-    def _(g):
-        for half in range(AK // NG):
-            j = g * (AK // NG) + half
-            s, wide = attend(j, near_slots)
-            top = jnp.max(s, axis=1, keepdims=True)
-            p = jnp.exp2(s - top).astype(bf16)
-            o = dot(p, wide)
-            acc[j] = o[:, :AD]
-            lsum[j] = o[:, AD:]
-            mtop[j] = jnp.broadcast_to(top, (ratio * TOK, AD))
-        pass_on(g)
-
-    arrived(0)
-    arrived(6)
 
     @pl.loop(0, AK)
     def _(j):
-        s, wide = attend(j, far_slots)
-        before = mtop[j]
-        top = jnp.maximum(before, jnp.max(s, axis=1, keepdims=True))
-        p = jnp.exp2(s - jnp.concatenate([top] * len(far_slots), axis=1)).astype(bf16)
-        o = dot(p, wide)
-        fade = jnp.exp2(before - top)
-        total = lsum[j] * fade + o[:, AD:]
-        out = ((acc[j] * fade + o[:, :AD]) / total).astype(bf16)
+        acc[j], lsum[j], mtop[j] = fold(j, near_slots)
+
+        @pl.when(j % 2 == 1)
+        def _():
+            pass_on(j // 2)
+
+
+    @pl.when(even & (b >= REACH))
+    def _():
+        for copy in half_kv(b):
+            copy.wait_recv()
+        kbuf[0, :HALF, :] = abuf[NG - 2, HALF:, :]
+        vbuf[0, :HALF, :] = abuf[NG - 1, HALF:, :]
+
+    @pl.when(odd)
+    def _():
+        arrived(6)
+
+    @pl.loop(0, AK)
+    def _(j):
+        weighted_sum, total, _ = fold(j, far_slots)
+        out = (weighted_sum / total).astype(bf16)
         square = jnp.zeros((TOK, AD), f32)
         for r in range(ratio):
             piece = out[r * TOK : (r + 1) * TOK]
@@ -499,18 +601,12 @@
     def _():
         scale_copy().wait_recv()
 
-    def unpack(raw):
-        built = dot(raw[HALF:, :N], raw[:HALF, :], TN)
-        return jnp.where(rows_in > 0.5, built, raw.astype(f32)).astype(bf16)
-
     @pl.loop(0, NG)
     def _(g):
         c_grp = c_ref[:, pl.ds(pl.multiple_of(g * N, N), N)]
 
         @pl.when(even)
         def _():
-            near_part = dot(c_grp, unpack(abuf[g]))
-
             @pl.when(b >= 4)
             def _():
                 remote(hbuf.at[g], hbuf.at[g], h_send.at[g], h_recv.at[g], b).wait_recv()
@@ -520,23 +616,20 @@
             seen = half.astype(f32)
             seen = jnp.concatenate([seen, jnp.zeros_like(seen)], axis=0)
             far_part = jnp.where(rows_before > 0.5, dot(c_grp, built), seen)
-            reach[...] = near_part + far_part * sbuf[g]
+            reach[...] = far_part * sbuf[g]
 
         @pl.when(odd)
         def _():
-            near_part = dot(c_grp, abuf[g])
-
             @pl.when(b >= 3)
             def _():
                 remote(bbuf.at[g], bbuf.at[g], rel1.at[g], b_recv.at[g], b).wait_recv()
 
-            reach[...] = near_part + dot(c_grp, unpack(bbuf[g])) * sbuf[g]
+            reach[...] = dot(c_grp, abuf[g]) + dot(c_grp, unpack(bbuf[g])) * sbuf[g]
 
         reached = reach[...]
         lanes = pl.ds(pl.multiple_of(g * GW, GW), GW)
         result = res[g] + reached * fx[g]
-        z = gate_ref[:, lanes].astype(f32)
-        gated = result * (z / (1.0 + jnp.exp(-z)))
+        gated = result * lift[g]
         square = jnp.sum(gated * gated, axis=1, keepdims=True) * (1.0 / GW)
         mixed = (gated * lax.rsqrt(square + norm_eps) * gain_ref[:, lanes]).astype(bf16)
         mamba_ref[:, lanes] = mixed
@@ -618,6 +711,7 @@
 
     @pl.when(even & bwd2)
     def _():
+        near_head_copy().wait_send()
         head_copy().wait_send()
 
     @pl.when(even & bwd1)
@@ -681,6 +775,7 @@
         V((HALF, NG * N), bf16),
         V((NG, HALF, GW), bf16),
         V((TOK, GW), f32),
+        V((NG, TOK, GW), f32),
         V((NG, 1, GW), f32),
         V((NG, N, GW), bf16),
         V((NG, N, GW), f32),
@@ -713,6 +808,7 @@
         D((NG,)),
         D,
         D,
+        D,
         D((near + n_row * n_dp,)),
         D((near + n_row * n_dp,)),
         D((7,)),

time: 66.5 us -> 64.2 us (0.965)
  Pallas kernels: 65.7 us -> 63.4 us
    pallas_call x1, Pallas kernels: 64.3 us -> 62 us  [shards(): pl.pallas_call(functools.partial(body, n_dp, n_ctx, near), out_shape=(plt...]
where the time goes in v4:
time: 64.2 us; the launch traced here: 64 us
  Pallas kernels  63.4 us (99%)
    pallas_call x1, Pallas kernels, shards(): pl.pallas_call(functools.partial(body, n_dp, n_ctx, near), out_shape=(plt...  62 us
    pallas_call x1, Pallas kernels, shards(): pl.pallas_call(put_out, out_shape=tuple((jax.ShapeDtypeStruct(r.shape, r....  1.35 us

profile of v4, /device:TPU:1, one launch (start us, length us, event | category | flops | bytes accessed | tf_op | source)
XLA Modules:
  0.0 64.0 jit_solution(12316896072416482904)
XLA Ops:
  0.6 62.0 %mixers.1 = (bf16[128,4096]{1,0:T(8,128)(2,1)S(1)}, bf16[128,4096]{1,0:T(8,128)(2,1)S(1)}, f32[2,2]{1,0:T(2,128)S(1)}) custom-call(s32[1,64]{1,0:T(1,128)} %starts_ref.1, s32[1,64]{1,0:T(1,128)} %ends_ref.1, s32[1,64]{1,0:T(1,128)} %modes_ref.1, bf16[128,4096]{1,0:T(8,128)(2,1)} %bitcast.11, f32[64,128]{1,0:T(8,128)} %bitcast.18, bf16[128,512]{1,0:T(8,128)(2,1)} %bitcast.16, ...), custom_call_target="tpu_custom_call" | custom-call | tf_op jit(solution)/shard_map/mixers/pallas_call | solution.py:816
  62.7 1.3 %put_out.1 = (bf16[128,4096]{1,0:T(8,128)(2,1)}, bf16[128,4096]{1,0:T(8,128)(2,1)}, f32[2,2]{1,0:T(2,128)}) custom-call(bf16[128,4096]{1,0:T(8,128)(2,1)S(1)} %get-tuple-element.9.refs_0_, bf16[128,4096]{1,0:T(8,128)(2,1)S(1)} %get-tuple-element.10.refs_1_, f32[2,2]{1,0:T(2,128)S(1)} %get-tuple-element.11.refs_2_), custom_call_target="tpu_custom_call" | custom-call | tf_op jit(solution)/shard_map/put_out/pallas_call | solution.py:832

commit v5 on v4

--- a/solution.py
+++ b/solution.py
@@ -80,6 +80,8 @@
     sbuf,
     ebuf,
     ewide,
+    elow,
+    alow,
     tbuf,
     tsend,
     fx,
@@ -101,6 +103,8 @@
     kv_recv,
     st_send,
     a_recv,
+    low_send,
+    low_recv,
     b_recv,
     s_send,
     s_recv,
@@ -166,8 +170,6 @@
             )
         )
     ]
-    for load in loads:
-        load.start()
 
     pl.semaphore_wait(barrier, count)
 
@@ -237,6 +239,8 @@
                 copy.wait_recv()
 
     start(sends)
+    for load in loads:
+        load.start()
 
     def head_copy():
         return remote(c_hbm.at[:HALF], chead, ch_send, ch_recv, b - 2)
@@ -337,6 +341,9 @@
     def state_copy(g):
         return remote(ebuf.at[g], abuf.at[g], st_send.at[g], a_recv.at[g], b + 1)
 
+    def low_copy(g):
+        return remote(elow.at[g], alow.at[g], low_send.at[g], low_recv.at[g], b + 1)
+
     def scale_copy():
         return remote(tsend, sbuf, s_send, s_recv, b + 1)
 
@@ -364,7 +371,9 @@
 
         @pl.when(even)
         def _():
+            elow[g] = (e - ebuf[g].astype(f32)).astype(bf16)
             state_copy(g).start()
+            low_copy(g).start()
 
     @pl.when(even)
     def _():
@@ -382,7 +391,8 @@
 
     def combine(g):
         state_copy(g).wait_recv()
-        state = ewide[g] + tbuf[g] * abuf[g].astype(f32)
+        low_copy(g).wait_recv()
+        state = ewide[g] + tbuf[g] * (abuf[g].astype(f32) + alow[g].astype(f32))
         top = wtail[g].astype(f32)
         b_rows = b_ref[HALF:, g * N : (g + 1) * N].astype(f32)
         low = jnp.concatenate([b_rows, top[:, N:]], axis=1)
@@ -532,9 +542,12 @@
         over = remote(hsend.at[g], hbuf.at[g], h_send.at[g], h_recv.at[g], b + 2)
         return up, over
 
-    def unpack(raw):
-        built = dot(raw[HALF:, :N], raw[:HALF, :], TN)
-        return jnp.where(rows_in > 0.5, built, raw.astype(f32)).astype(bf16)
+    def through_rows(c_grp, b_rows, x_rows):
+        return dot(dot(c_grp, b_rows, NT).astype(bf16), x_rows)
+
+    def read_state(c_grp, raw):
+        by_rows = through_rows(c_grp, raw[HALF:, :N], raw[:HALF, :])
+        return jnp.where(rows_in > 0.5, by_rows, dot(c_grp, raw))
 
     def pass_on(g):
         @pl.when(even & bwd1)
@@ -558,7 +571,7 @@
             raw = abuf[g]
             upper = raw[:HALF].astype(f32)
             brief = jnp.concatenate([upper, jnp.zeros_like(upper)], axis=0)
-            got = jnp.where(short_in > 0.5, brief, dot(c_grp, unpack(raw)))
+            got = jnp.where(short_in > 0.5, brief, read_state(c_grp, raw))
             res[g] = res[g] + got * fx[g]
 
     @pl.when(even & fwd2)
@@ -612,10 +625,9 @@
                 remote(hbuf.at[g], hbuf.at[g], h_send.at[g], h_recv.at[g], b).wait_recv()
 
             half = hbuf[g, :, :GW]
-            built = dot(hbuf[g, :, GW:], half, TN).astype(bf16)
             seen = half.astype(f32)
             seen = jnp.concatenate([seen, jnp.zeros_like(seen)], axis=0)
-            far_part = jnp.where(rows_before > 0.5, dot(c_grp, built), seen)
+            far_part = jnp.where(rows_before > 0.5, through_rows(c_grp, hbuf[g, :, GW:], half), seen)
             reach[...] = far_part * sbuf[g]
 
         @pl.when(odd)
@@ -624,7 +636,11 @@
             def _():
                 remote(bbuf.at[g], bbuf.at[g], rel1.at[g], b_recv.at[g], b).wait_recv()
 
-            reach[...] = dot(c_grp, abuf[g]) + dot(c_grp, unpack(bbuf[g])) * sbuf[g]
+            reach[...] = (
+                dot(c_grp, abuf[g])
+                + dot(c_grp, alow[g])
+                + read_state(c_grp, bbuf[g]) * sbuf[g]
+            )
 
         reached = reach[...]
         lanes = pl.ds(pl.multiple_of(g * GW, GW), GW)
@@ -708,6 +724,12 @@
         @pl.loop(0, NG)
         def _(g):
             state_copy(g).wait_send()
+
+    @pl.when(even)
+    def _():
+        @pl.loop(0, NG)
+        def _(g):
+            low_copy(g).wait_send()
 
     @pl.when(even & bwd2)
     def _():
@@ -779,6 +801,8 @@
         V((NG, 1, GW), f32),
         V((NG, N, GW), bf16),
         V((NG, N, GW), f32),
+        V((NG, N, GW), bf16),
+        V((NG, N, GW), bf16),
         V((NG, 1, GW), f32),
         V((NG, 1, GW), f32),
         V((NG, TOK, GW), f32),
@@ -798,6 +822,8 @@
         V((n_row * n_dp, 8, TOK), f32),
         D((7, 2)),
         D((7, 2)),
+        D((NG,)),
+        D((NG,)),
         D((NG,)),
         D((NG,)),
         D((NG,)),

time: 64.2 us -> 64.1 us (level)
  no operation moved by 1% of the time
where the time goes in v5:
time: 64.1 us; the launch traced here: 64 us
  Pallas kernels  63.3 us (99%)
    pallas_call x1, Pallas kernels, shards(): pl.pallas_call(functools.partial(body, n_dp, n_ctx, near), out_shape=(plt...  62 us
    pallas_call x1, Pallas kernels, shards(): pl.pallas_call(put_out, out_shape=tuple((jax.ShapeDtypeStruct(r.shape, r....  1.35 us

profile of v5, /device:TPU:1, one launch (start us, length us, event | category | flops | bytes accessed | tf_op | source)
XLA Modules:
  0.0 64.0 jit_solution(15135198250943884415)
XLA Ops:
  0.6 62.0 %mixers.1 = (bf16[128,4096]{1,0:T(8,128)(2,1)S(1)}, bf16[128,4096]{1,0:T(8,128)(2,1)S(1)}, f32[2,2]{1,0:T(2,128)S(1)}) custom-call(s32[1,64]{1,0:T(1,128)} %starts_ref.1, s32[1,64]{1,0:T(1,128)} %ends_ref.1, s32[1,64]{1,0:T(1,128)} %modes_ref.1, bf16[128,4096]{1,0:T(8,128)(2,1)} %bitcast.11, f32[64,128]{1,0:T(8,128)} %bitcast.18, bf16[128,512]{1,0:T(8,128)(2,1)} %bitcast.16, ...), custom_call_target="tpu_custom_call" | custom-call | tf_op jit(solution)/shard_map/mixers/pallas_call | solution.py:842
  62.6 1.3 %put_out.1 = (bf16[128,4096]{1,0:T(8,128)(2,1)}, bf16[128,4096]{1,0:T(8,128)(2,1)}, f32[2,2]{1,0:T(2,128)}) custom-call(bf16[128,4096]{1,0:T(8,128)(2,1)S(1)} %get-tuple-element.9.refs_0_, bf16[128,4096]{1,0:T(8,128)(2,1)S(1)} %get-tuple-element.10.refs_1_, f32[2,2]{1,0:T(2,128)S(1)} %get-tuple-element.11.refs_2_), custom_call_target="tpu_custom_call" | custom-call | tf_op jit(solution)/shard_map/put_out/pallas_call | solution.py:858
